TPU v7x, 32 devices: a whole 2x2x4 slice. The times are simulated.
32 devices in a mesh: dp: 16 (over z, y, core), mp: 2 (over x).
Axes of the slice: x: 2, y: 2, z: 4, core: 2. Of those that a mesh axis runs over, the one named last changes fastest.
Arguments:
- inputs: bfloat16 [64, 320, 1024], P('dp', 'mp'), may hold values from -6 to 6
- teacher: bfloat16 [64, 320, 1024], P('dp', 'mp'), may hold values from -6 to 6
- keep_mask: int32 [64, 320], P('dp'), may hold values from 0 to 1, as said below
- gain_attn: bfloat16 [1024], P('dp'), may hold values from 0.099609375 to 1.8984375
- qkv_weight: bfloat16 [1024, 3, 1024], P('dp', None, 'mp'), may hold values from -0.25 to 0.25
- out_weight: bfloat16 [1024, 1024], P('dp', 'mp'), may hold values from -0.5 to 0.5
- gain_mlp: bfloat16 [1024], P('dp'), may hold values from 0.099609375 to 1.8984375
- up_weight: bfloat16 [1024, 4096], P('dp', 'mp'), may hold values from -0.1875 to 0.1875
- down_weight: bfloat16 [1024, 4096], P('dp', 'mp'), may hold values from -0.125 to 0.125
Outputs:
- output: bfloat16 [64, 320, 1024], P('dp', 'mp')
- loss: float32 [], replicated
- input_grad: float32 [64, 320, 1024], P('dp', 'mp')
- gain_attn_grad: float32 [1024], P('dp')
- qkv_grad: float32 [1024, 3, 1024], P('dp', None, 'mp')
- out_grad: float32 [1024, 1024], P('dp', 'mp')
- gain_mlp_grad: float32 [1024], P('dp')
- up_grad: float32 [1024, 4096], P('dp', 'mp')
- down_grad: float32 [1024, 4096], P('dp', 'mp')
Inputs may be any that keep to these rules, and one draw needn't show every extreme that they name: `keep_mask`: the first 64 positions of every image are 1; how many of its other positions an image keeps varies from image to image and from draw to draw.
All inputs are finite; a program needn't handle non-finite values.
Results may differ from a plain program's by a relative error of at most 0.009.
The roundings to bfloat16 on the way count: a program that leaves them out, or rounds other values in their place, can miss the bound.
Values may be sent and summed in bfloat16 or wider, within the bound.
A program may use at most 96 MiB of HBM per device.

v0:
```python
import jax
import jax.numpy as jnp
from jax import lax
from jax.sharding import PartitionSpec as P

HDIM = 64
MICRO = 2


norm_epsilon = 1e-06


def normalize(values):
    centre = values - jnp.mean(values, axis=-1, keepdims=True)
    spread = jnp.mean(centre * centre, axis=-1, keepdims=True)
    scaled = lax.rsqrt(spread + norm_epsilon)
    return (centre * scaled, scaled)


def norm_back(grad_out, unit_rows, scaled, gain_values):
    grad_scaled = grad_out * gain_values
    first = jnp.mean(grad_scaled, axis=-1, keepdims=True)
    second = jnp.mean(grad_scaled * unit_rows, axis=-1, keepdims=True)
    return scaled * (grad_scaled - first - unit_rows * second)


def exact_gelu(values):
    return jax.nn.gelu(values, approximate=False)


def full_rows(piece):
    return lax.all_gather(piece, "mp", axis=1, tiled=True)


def row_sums(partial_rows):
    return lax.psum_scatter(partial_rows, "mp", scatter_dimension=1, tiled=True)


def full_grads(piece):
    return lax.all_gather(piece, "mp", axis=1, tiled=True)


def sum_grads(partial_rows):
    return lax.psum_scatter(partial_rows, "mp", scatter_dimension=1, tiled=True)


def split_heads(projected):
    image_count, seq_length = (projected.shape[0], projected.shape[1])
    head_count = projected.shape[3] // HDIM
    queries = projected[:, :, 0].reshape(image_count, seq_length, head_count, HDIM)
    key_rows = projected[:, :, 1].reshape(image_count, seq_length, head_count, HDIM)
    value_rows = projected[:, :, 2].reshape(image_count, seq_length, head_count, HDIM)
    return (queries, key_rows, value_rows)


def masked_scores(queries, key_rows, allowed):
    scores = jnp.einsum(
        "bqhe,bkhe->bhqk", queries, key_rows, preferred_element_type=jnp.float32
    ) * HDIM ** (-0.5)
    return jnp.where(allowed, scores, -1e30)


def attend(projected, allowed):
    queries, key_rows, value_rows = split_heads(projected)
    scores = masked_scores(queries, key_rows, allowed)
    maximum = jnp.max(scores, axis=-1, keepdims=True)
    raised = jnp.exp(scores - maximum)
    normaliser = jnp.sum(raised, axis=-1, keepdims=True)
    weights_soft = (raised / normaliser).astype(jnp.bfloat16)
    log_total = maximum + jnp.log(normaliser)
    mixture = jnp.einsum(
        "bhqk,bkhe->bqhe", weights_soft, value_rows, preferred_element_type=jnp.float32
    )
    shaped = mixture.reshape(projected.shape[0], projected.shape[1], projected.shape[3])
    return (shaped.astype(jnp.bfloat16), log_total)


def attend_back(projected, allowed, log_total, grad_heads):
    queries, key_rows, value_rows = split_heads(projected)
    scores = masked_scores(queries, key_rows, allowed)
    weights_soft = jnp.exp(scores - log_total)
    grad_mix = grad_heads.reshape(queries.shape)
    grad_weights = jnp.einsum(
        "bqhe,bkhe->bhqk", grad_mix, value_rows, preferred_element_type=jnp.float32
    )
    inner = jnp.sum(grad_weights * weights_soft, axis=-1, keepdims=True)
    grad_scores = (weights_soft * (grad_weights - inner)).astype(jnp.bfloat16)
    grad_query = jnp.einsum(
        "bhqk,bkhe->bqhe", grad_scores, key_rows, preferred_element_type=jnp.float32
    ) * HDIM ** (-0.5)
    grad_key = jnp.einsum(
        "bhqk,bqhe->bkhe", grad_scores, queries, preferred_element_type=jnp.float32
    ) * HDIM ** (-0.5)
    grad_value = jnp.einsum(
        "bhqk,bqhe->bkhe",
        weights_soft.astype(jnp.bfloat16),
        grad_mix,
        preferred_element_type=jnp.float32,
    )
    stacked = jnp.stack(
        [
            grad_query.astype(jnp.bfloat16),
            grad_key.astype(jnp.bfloat16),
            grad_value.astype(jnp.bfloat16),
        ],
        axis=2,
    )
    return stacked.reshape(projected.shape)


def per_device(
    inputs, teacher, keep_mask, gain_attn, qkv_weight, out_weight, gain_mlp, up_weight, down_weight
):
    owned = (gain_attn, gain_mlp, qkv_weight, out_weight, up_weight, down_weight)
    half_len = inputs.shape[1]
    offset = lax.axis_index("mp") * half_len
    keep_local = lax.dynamic_slice_in_dim(keep_mask, offset, half_len, 1)
    valid_total = lax.psum(jnp.sum(keep_local).astype(jnp.float32), ("dp", "mp"))
    token_total = inputs.shape[0] * lax.axis_size("dp") * half_len * lax.axis_size("mp")
    loss_factor = 2.0 * token_total / valid_total
    per_micro = inputs.shape[0] // MICRO
    summed = tuple(
        (
            jnp.zeros((piece.shape[0] * lax.axis_size("dp"),) + piece.shape[1:], jnp.float32)
            for piece in owned
        )
    )
    outputs = []
    input_grads = []
    loss_local = jnp.zeros((), jnp.float32)
    for micro_step in range(MICRO):
        first_image = micro_step * per_micro
        field_in = inputs[first_image : first_image + per_micro].astype(jnp.float32)
        target = teacher[first_image : first_image + per_micro].astype(jnp.float32)
        keep_rows = keep_local[first_image : first_image + per_micro].astype(jnp.float32)[
            :, :, None
        ]
        allowed = (keep_mask[first_image : first_image + per_micro] > 0)[:, None, None, :]
        forward_set = (
            lax.all_gather(gain_attn, "dp", axis=0, tiled=True),
            lax.all_gather(gain_mlp, "dp", axis=0, tiled=True),
            lax.all_gather(qkv_weight, "dp", axis=0, tiled=True),
            lax.all_gather(out_weight, "dp", axis=0, tiled=True),
            lax.all_gather(up_weight, "dp", axis=0, tiled=True),
            lax.all_gather(down_weight, "dp", axis=0, tiled=True),
        )
        gain_one = forward_set[0].astype(jnp.float32)
        gain_two = forward_set[1].astype(jnp.float32)
        w_qkv, w_out, w_up, w_down = (
            forward_set[2],
            forward_set[3],
            forward_set[4],
            forward_set[5],
        )
        unit_one, scaled_one = normalize(field_in)
        normed_full = full_rows((unit_one * gain_one).astype(jnp.bfloat16))
        projected = jnp.einsum(
            "bsd,dcf->bscf", normed_full, w_qkv, preferred_element_type=jnp.float32
        ).astype(jnp.bfloat16)
        heads_out, log_total = attend(projected, allowed)
        attended = row_sums(
            jnp.einsum("bsf,df->bsd", heads_out, w_out, preferred_element_type=jnp.float32)
        )
        middle = field_in + attended
        unit_two, scaled_two = normalize(middle)
        normed_wide = full_rows((unit_two * gain_two).astype(jnp.bfloat16))
        hidden_in = jnp.einsum("bsd,df->bsf", normed_wide, w_up, preferred_element_type=jnp.float32)
        activated, gelu_back = jax.vjp(exact_gelu, hidden_in)
        hidden = activated.astype(jnp.bfloat16)
        branch = row_sums(
            jnp.einsum("bsf,df->bsd", hidden, w_down, preferred_element_type=jnp.float32)
        )
        result = middle + branch
        outputs.append((result * keep_rows).astype(jnp.bfloat16))
        error = result - target
        loss_local = loss_local + jnp.sum(
            keep_rows * jnp.mean(error * error, axis=-1, keepdims=True)
        )
        grad_result = loss_factor * keep_rows * error
        backward_set = (
            lax.all_gather(gain_attn, "dp", axis=0, tiled=True),
            lax.all_gather(gain_mlp, "dp", axis=0, tiled=True),
            lax.all_gather(qkv_weight, "dp", axis=0, tiled=True),
            lax.all_gather(out_weight, "dp", axis=0, tiled=True),
            lax.all_gather(up_weight, "dp", axis=0, tiled=True),
            lax.all_gather(down_weight, "dp", axis=0, tiled=True),
        )
        w_qkv, w_out, w_up, w_down = (
            backward_set[2],
            backward_set[3],
            backward_set[4],
            backward_set[5],
        )
        grad_branch = full_grads(grad_result.astype(jnp.bfloat16))
        grad_hidden = jnp.einsum(
            "bsd,df->bsf", grad_branch, w_down, preferred_element_type=jnp.float32
        )
        down_part = jnp.einsum(
            "bsd,bsf->df", grad_branch, hidden, preferred_element_type=jnp.float32
        )
        grad_pre = gelu_back(grad_hidden)[0].astype(jnp.bfloat16)
        up_part = jnp.einsum(
            "bsd,bsf->df", normed_wide, grad_pre, preferred_element_type=jnp.float32
        )
        grad_normed_two = sum_grads(
            jnp.einsum("bsf,df->bsd", grad_pre, w_up, preferred_element_type=jnp.float32)
        )
        gain_mlp_part = jnp.sum(grad_normed_two * unit_two, axis=(0, 1))
        grad_middle = grad_result + norm_back(grad_normed_two, unit_two, scaled_two, gain_two)
        grad_attended = full_grads(grad_middle.astype(jnp.bfloat16))
        grad_heads = jnp.einsum(
            "bsd,df->bsf", grad_attended, w_out, preferred_element_type=jnp.float32
        ).astype(jnp.bfloat16)
        out_part = jnp.einsum(
            "bsd,bsf->df", grad_attended, heads_out, preferred_element_type=jnp.float32
        )
        grad_projected = attend_back(projected, allowed, log_total, grad_heads)
        qkv_part = jnp.einsum(
            "bsd,bscf->dcf", normed_full, grad_projected, preferred_element_type=jnp.float32
        )
        grad_normed_one = sum_grads(
            jnp.einsum("bscf,dcf->bsd", grad_projected, w_qkv, preferred_element_type=jnp.float32)
        )
        gain_attn_part = jnp.sum(grad_normed_one * unit_one, axis=(0, 1))
        input_grads.append(grad_middle + norm_back(grad_normed_one, unit_one, scaled_one, gain_one))
        fresh = (gain_attn_part, gain_mlp_part, qkv_part, out_part, up_part, down_part)
        summed = tuple((current + added for current, added in zip(summed, fresh)))
    summed = (
        lax.psum_scatter(summed[0], "dp", scatter_dimension=0, tiled=True),
        lax.psum_scatter(summed[1], "dp", scatter_dimension=0, tiled=True),
        lax.psum_scatter(summed[2], "dp", scatter_dimension=0, tiled=True),
        lax.psum_scatter(summed[3], "dp", scatter_dimension=0, tiled=True),
        lax.psum_scatter(summed[4], "dp", scatter_dimension=0, tiled=True),
        lax.psum_scatter(summed[5], "dp", scatter_dimension=0, tiled=True),
    )
    gain_sums = lax.psum((summed[0], summed[1]), "mp")
    loss = lax.psum(loss_local, ("dp", "mp")) / valid_total
    output = jnp.concatenate(outputs, axis=0)
    input_grad = jnp.concatenate(input_grads, axis=0)
    return (
        output,
        loss,
        input_grad,
        gain_sums[0],
        summed[2],
        summed[3],
        gain_sums[1],
        summed[4],
        summed[5],
    )


def solution(mesh):
    in_specs = (
        P("dp", "mp", None),
        P("dp", "mp", None),
        P("dp", None),
        P("dp"),
        P("dp", None, "mp"),
        P("dp", "mp"),
        P("dp"),
        P("dp", "mp"),
        P("dp", "mp"),
    )
    out_specs = (
        P("dp", "mp", None),
        P(),
        P("dp", "mp", None),
        P("dp"),
        P("dp", None, "mp"),
        P("dp", "mp"),
        P("dp"),
        P("dp", "mp"),
        P("dp", "mp"),
    )
    return jax.shard_map(
        per_device, mesh=mesh, in_specs=in_specs, out_specs=out_specs, check_vma=False
    )
```

profile of v0, /device:TPU:0, one launch (start us, length us, event | category | flops | bytes accessed | tf_op | source)
XLA Modules:
  0.0 1163.0 jit_solution(9195493048433533163)
XLA Ops:
  10.9 34.9 %all-reduce.6 = (bf16[1024]{0:T(1024)(128)(2,1)S(1)}, bf16[1024]{0:T(1024)(128)(2,1)S(1)}) all-reduce(bf16[1024]{0:T(1024)(128)(2,1)S(1)} %dynamic-update-slice, bf16[1024]{0:T(1024)(128)(2,1)S(1)} %dynamic-update-slice.1), channel_id=1, replica_groups=mesh['dp'=16,'mp'=2] {'dp'}, use_global_device_ids=true, to_apply=%add | all-reduce | flops 2048 | bytes 8192
  54.3 19.5 %all-gather.13.cloned.1.call-done = bf16[2,320,1024]{2,1,0:T(8,128)(2,1)} async-done(((bf16[2,160,1024]{2,1,0:T(8,128)(2,1)}), bf16[2,320,1024]{2,1,0:T(8,128)(2,1)}) %all-gather.13.cloned.1.call-update) | async-done | bytes 1310736 | tf_op jit(solution)/shard_map/all_gather | solution.py:32
  73.8 47.4 %all-gather.15.cloned.1.call-done = bf16[1024,3,512]{2,0,1:T(8,128)(2,1)} async-done(((bf16[64,3,512]{2,0,1:T(8,128)(2,1)}), bf16[1024,3,512]{2,0,1:T(8,128)(2,1)}) %all-gather.15.cloned.1.call-update) | async-done | bytes 3145744 | tf_op jit(solution)/shard_map/all_gather | solution.py:142
  121.2 4.5 fusion.54
  134.9 25.3 %all-gather.17.cloned.1.call-done = bf16[1024,512]{1,0:T(8,128)(2,1)} async-done(((bf16[64,512]{1,0:T(8,128)(2,1)}), bf16[1024,512]{1,0:T(8,128)(2,1)}) %all-gather.17.cloned.1.call-update) | async-done | bytes 1048592 | tf_op jit(solution)/shard_map/all_gather | solution.py:143
  164.4 20.3 %all-gather.25.cloned.1.call-done = bf16[2,320,1024]{2,1,0:T(8,128)(2,1)} async-done(((bf16[2,160,1024]{2,1,0:T(8,128)(2,1)}), bf16[2,320,1024]{2,1,0:T(8,128)(2,1)}) %all-gather.25.cloned.1.call-update) | async-done | bytes 1310736 | tf_op jit(solution)/shard_map/all_gather | solution.py:32
  184.8 4.5 fusion.57
  202.1 23.0 %reduce-scatter.13.cloned.1.call-done = f32[2,160,1024]{2,1,0:T(8,128)} async-done(((f32[2,320,1024]{2,1,0:T(8,128)}), f32[2,160,1024]{2,1,0:T(8,128)}) %reduce-scatter.13.cloned.1.call-update) | async-done | bytes 1310736 | tf_op jit(solution)/shard_map/reduce_scatter | solution.py:36
  225.1 39.8 %reduce-scatter.17.cloned.1.call-done = f32[2,160,1024]{2,1,0:T(8,128)} async-done(((f32[2,320,1024]{2,1,0:T(8,128)}), f32[2,160,1024]{2,1,0:T(8,128)}) %reduce-scatter.17.cloned.1.call-update) | async-done | bytes 1310736 | tf_op jit(solution)/shard_map/reduce_scatter | solution.py:36
  271.3 46.3 %all-gather.21.cloned.1.call-done = bf16[1024,2048]{1,0:T(8,128)(2,1)} async-done(((bf16[64,2048]{1,0:T(8,128)(2,1)}), bf16[1024,2048]{1,0:T(8,128)(2,1)}) %all-gather.21.cloned.1.call-update) | async-done | bytes 4194320 | tf_op jit(solution)/shard_map/all_gather | solution.py:144
  317.6 24.9 %all-gather.19.cloned.1.call-done = bf16[2,320,1024]{2,1,0:T(8,128)(2,1)} async-done(((bf16[2,160,1024]{2,1,0:T(8,128)(2,1)}), bf16[2,320,1024]{2,1,0:T(8,128)(2,1)}) %all-gather.19.cloned.1.call-update) | async-done | bytes 1310736 | tf_op jit(solution)/shard_map/all_gather | solution.py:32
  342.5 6.9 fusion.107
  351.7 12.9 %multiply_convert_fusion.3 = (bf16[2,320,2048]{2,1,0:T(8,128)(2,1)}, f32[2,320,2048]{2,1,0:T(8,128)}) fusion(f32[2,320,2048]{2,1,0:T(8,128)S(1)} %get-tuple-element.87, u8[320,2048]{1,0:T(8,128)(4,1)S(1)} %get-tuple-element.10, u8[320,2048]{1,0:T(8,128)(4,1)S(1)} %get-tuple-element.9), kind=kLoop, calls=%fused_computation.47 | loop fusion | flops 91750400 | bytes 14417920 | tf_op jit(solution)/shard_map/convert_element_type | solution.py:169
  364.6 30.8 %all-gather.23.cloned.1.call-done = bf16[1024,2048]{1,0:T(8,128)(2,1)} async-done(((bf16[64,2048]{1,0:T(8,128)(2,1)}), bf16[1024,2048]{1,0:T(8,128)(2,1)}) %all-gather.23.cloned.1.call-update) | async-done | bytes 4194320 | tf_op jit(solution)/shard_map/all_gather | solution.py:145
  395.4 7.4 fusion.22
  403.0 16.6 %all-gather.27.cloned.1.call-done = bf16[2,320,1024]{2,1,0:T(8,128)(2,1)} async-done(((bf16[2,160,1024]{2,1,0:T(8,128)(2,1)}), bf16[2,320,1024]{2,1,0:T(8,128)(2,1)}) %all-gather.27.cloned.1.call-update) | async-done | bytes 1310736 | tf_op jit(solution)/shard_map/all_gather | solution.py:32
  419.6 6.9 fusion.108
  426.5 12.8 %multiply_convert_fusion.2 = (bf16[2,320,2048]{2,1,0:T(8,128)(2,1)S(1)}, f32[2,320,2048]{2,1,0:T(8,128)}) fusion(f32[2,320,2048]{2,1,0:T(8,128)S(1)} %get-tuple-element.86, u8[320,2048]{1,0:T(8,128)(4,1)S(1)} %get-tuple-element.12, u8[320,2048]{1,0:T(8,128)(4,1)S(1)} %get-tuple-element.11), kind=kLoop, calls=%fused_computation.34 | loop fusion | flops 91750400 | bytes 14417920 | tf_op jit(solution)/shard_map/convert_element_type | solution.py:169
  440.9 4.4 fusion.20
  446.7 39.7 %psum.29 = f32[]{:T(128)} all-reduce(f32[]{:T(128)S(6)} %convert_element_type.181), channel_id=1, replica_groups=mesh['dp'=16,'mp'=2] {'dp','mp'}, use_global_device_ids=true, to_apply=%region_22.23 | all-reduce | flops 1 | bytes 8 | tf_op jit(solution)/shard_map/psum | solution.py:118
  487.2 13.4 %reduce-scatter.19.cloned.1.call-done = f32[2,160,1024]{2,1,0:T(8,128)} async-done(((f32[2,320,1024]{2,1,0:T(8,128)}), f32[2,160,1024]{2,1,0:T(8,128)}) %reduce-scatter.19.cloned.1.call-update) | async-done | bytes 1310736 | tf_op jit(solution)/shard_map/reduce_scatter | solution.py:36
  505.1 23.6 %all-gather.29.cloned.1.call-done = bf16[2,320,1024]{2,1,0:T(8,128)(2,1)} async-done(((bf16[2,160,1024]{2,1,0:T(8,128)(2,1)}), bf16[2,320,1024]{2,1,0:T(8,128)(2,1)}) %all-gather.29.cloned.1.call-update) | async-done | bytes 1310736 | tf_op jit(solution)/shard_map/all_gather | solution.py:40
  528.7 10.0 add_convert_fusion.1
  540.2 4.4 fusion.26
  544.7 9.7 all-gather.33.cloned.1.call-done
  554.4 10.0 add_convert_fusion
  565.9 4.4 fusion.24
  570.8 23.3 %reduce-scatter.21.cloned.1.call-done = f32[2,160,1024]{2,1,0:T(8,128)} async-done(((f32[2,320,1024]{2,1,0:T(8,128)}), f32[2,160,1024]{2,1,0:T(8,128)}) %reduce-scatter.21.cloned.1.call-update) | async-done | bytes 1310736 | tf_op jit(solution)/shard_map/reduce_scatter | solution.py:44
  594.1 39.8 %reduce-scatter.25.cloned.1.call-done = f32[2,160,1024]{2,1,0:T(8,128)} async-done(((f32[2,320,1024]{2,1,0:T(8,128)}), f32[2,160,1024]{2,1,0:T(8,128)}) %reduce-scatter.25.cloned.1.call-update) | async-done | bytes 1310736 | tf_op jit(solution)/shard_map/reduce_scatter | solution.py:44
  633.9 4.4 multiply_reduce_fusion.2
  645.0 20.0 %all-gather.35.cloned.1.call-done = bf16[2,320,1024]{2,1,0:T(8,128)(2,1)} async-done(((bf16[2,160,1024]{2,1,0:T(8,128)(2,1)}), bf16[2,320,1024]{2,1,0:T(8,128)(2,1)}) %all-gather.35.cloned.1.call-update) | async-done | bytes 1310736 | tf_op jit(solution)/shard_map/all_gather | solution.py:40
  670.3 7.2 multiply_reduce_fusion
  696.1 6.1 fusion.63
  705.1 5.3 fusion.80
  711.5 5.2 multiply_reduce_fusion.1
  716.8 4.7 multiply_convert_fusion.1
  729.1 6.3 fusion.60
  740.7 5.8 fusion.137
  746.5 6.1 bitcast_add_fusion.1
  754.3 5.0 fusion.138
  759.3 6.0 bitcast_add_fusion
  770.9 4.8 bitcast_add_fusion.2
  779.5 39.3 %psum.28 = f32[]{:T(128)} all-reduce(f32[]{:T(128)S(6)} %add.141), channel_id=1, replica_groups=mesh['dp'=16,'mp'=2] {'dp','mp'}, use_global_device_ids=true, to_apply=%region_20.21 | all-reduce | flops 1 | bytes 8 | tf_op jit(solution)/shard_map/psum | solution.py:237
  825.4 32.9 %all-reduce.4 = (f32[1024]{0:T(1024)S(1)}, f32[1024]{0:T(1024)S(1)}) all-reduce(f32[1024]{0:T(1024)S(1)} %add.148, f32[1024]{0:T(1024)S(1)} %add.151), channel_id=10, replica_groups=mesh['dp'=16,'mp'=2] {'dp'}, use_global_device_ids=true, to_apply=%region_39.40.clone | all-reduce | flops 2048 | bytes 16384
  858.4 5.4 all-reduce.5
  868.6 86.5 %reduce-scatter.33.cloned.1.call-done = f32[64,2048]{1,0:T(8,128)} async-done(((f32[1024,2048]{1,0:T(8,128)}), f32[64,2048]{1,0:T(8,128)}) %reduce-scatter.33.cloned.1.call-update) | async-done | bytes 524304 | tf_op jit(solution)/shard_map/reduce_scatter | solution.py:233
  955.1 109.6 %reduce-scatter.35.cloned.1.call-done = f32[64,2048]{1,0:T(8,128)} async-done(((f32[1024,2048]{1,0:T(8,128)}), f32[64,2048]{1,0:T(8,128)}) %reduce-scatter.35.cloned.1.call-update) | async-done | bytes 524304 | tf_op jit(solution)/shard_map/reduce_scatter | solution.py:234
  1064.7 89.9 %reduce-scatter.29.cloned.1.call-done = f32[64,3,512]{2,0,1:T(8,128)} async-done(((f32[1024,3,512]{2,0,1:T(8,128)}), f32[64,3,512]{2,0,1:T(8,128)}) %reduce-scatter.29.cloned.1.call-update) | async-done | bytes 393232 | tf_op jit(solution)/shard_map/reduce_scatter | solution.py:231
  (268 shorter events, 122.7 us)
Async XLA Ops:
  7.2 47.1 %copy-start.47 = (s32[4,320]{1,0:T(4,128)S(1)}, s32[4,320]{1,0:T(4,128)}, u32[]{:S(2)}) copy-start(s32[4,320]{1,0:T(4,128)} %param.11) | copy-start | bytes 15364
  7.2 66.6 %all-gather.13.cloned.1.call-start = ((), (), s32[]{:S(2)}) async-start(), calls=%async_computation.12 | async-start | bytes 1966080 | tf_op jit(solution)/shard_map/all_gather | solution.py:32
  52.1 69.1 %all-gather.15.cloned.1.call-start = ((), (), s32[]{:S(2)}) async-start(), calls=%async_computation.13 | async-start | bytes 3342336 | tf_op jit(solution)/shard_map/all_gather | solution.py:142
  52.9 107.3 %all-gather.17.cloned.1.call-start = ((), (), s32[]{:S(2)}) async-start(), calls=%async_computation.14 | async-start | bytes 1114112 | tf_op jit(solution)/shard_map/all_gather | solution.py:143
  53.6 131.2 %all-gather.25.cloned.1.call-start = ((), (), s32[]{:S(2)}) async-start(), calls=%async_computation.20 | async-start | bytes 1966080 | tf_op jit(solution)/shard_map/all_gather | solution.py:32
  54.2 170.9 %reduce-scatter.13.cloned.1.call-start = ((), (), s32[]{:S(2)}) async-start(), calls=%async_computation.15 | async-start | bytes 3932160 | tf_op jit(solution)/shard_map/reduce_scatter | solution.py:36
  134.9 54.4 %copy-start.30 = (bf16[2,8,64,320]{3,2,1,0:T(8,128)(2,1)}, bf16[2,8,64,320]{3,2,1,0:T(8,128)(2,1)S(1)}, u32[]{:S(2)}) copy-start(bf16[2,8,64,320]{3,2,1,0:T(8,128)(2,1)S(1)} %fusion.79) | copy-start | bytes 1966084
  164.1 100.8 %reduce-scatter.17.cloned.1.call-start = ((), (), s32[]{:S(2)}) async-start(), calls=%async_computation.21 | async-start | bytes 3932160 | tf_op jit(solution)/shard_map/reduce_scatter | solution.py:36
  198.5 26.5 %copy-start.23 = (bf16[2,8,64,320]{3,2,1,0:T(8,128)(2,1)}, bf16[2,8,64,320]{3,2,1,0:T(8,128)(2,1)S(1)}, u32[]{:S(2)}) copy-start(bf16[2,8,64,320]{3,2,1,0:T(8,128)(2,1)S(1)} %fusion.78) | copy-start | bytes 1966084
  201.2 116.4 %all-gather.21.cloned.1.call-start = ((), (), s32[]{:S(2)}) async-start(), calls=%async_computation.17 | async-start | bytes 4456448 | tf_op jit(solution)/shard_map/all_gather | solution.py:144
  202.0 140.5 %all-gather.19.cloned.1.call-start = ((), (), s32[]{:S(2)}) async-start(), calls=%async_computation.16 | async-start | bytes 1966080 | tf_op jit(solution)/shard_map/all_gather | solution.py:32
  269.4 126.1 %all-gather.23.cloned.1.call-start = ((), (), s32[]{:S(2)}) async-start(), calls=%async_computation.18 | async-start | bytes 4456448 | tf_op jit(solution)/shard_map/all_gather | solution.py:145
  270.1 149.5 %all-gather.27.cloned.1.call-start = ((), (), s32[]{:S(2)}) async-start(), calls=%async_computation.22 | async-start | bytes 1966080 | tf_op jit(solution)/shard_map/all_gather | solution.py:32
  270.7 216.5 %reduce-scatter.15.cloned.1.call-start = ((), (), s32[]{:S(2)}) async-start(), calls=%async_computation.19 | async-start | bytes 3932160 | tf_op jit(solution)/shard_map/reduce_scatter | solution.py:36
  402.8 97.8 %reduce-scatter.19.cloned.1.call-start = ((), (), s32[]{:S(2)}) async-start(), calls=%async_computation.23 | async-start | bytes 3932160 | tf_op jit(solution)/shard_map/reduce_scatter | solution.py:36
  426.5 12.8 %copy-start.13 = (f32[2,320,2048]{2,1,0:T(8,128)}, f32[2,320,2048]{2,1,0:T(8,128)S(1)}, u32[]{:S(2)}) copy-start(f32[2,320,2048]{2,1,0:T(8,128)S(1)} %get-tuple-element.86) | copy-start | bytes 15728644
  426.5 14.3 %copy-start.57 = (bf16[1024,2048]{1,0:T(8,128)(2,1)S(1)}, bf16[1024,2048]{1,0:T(8,128)(2,1)}, u32[]{:S(2)}) copy-start(bf16[1024,2048]{1,0:T(8,128)(2,1)} %all-gather.23.cloned.1.call-done) | copy-start | bytes 12582916
  445.3 83.4 %all-gather.29.cloned.1.call-start = ((), (), s32[]{:S(2)}) async-start(), calls=%async_computation.24 | async-start | bytes 1966080 | tf_op jit(solution)/shard_map/all_gather | solution.py:40
  504.2 50.1 %all-gather.33.cloned.1.call-start = ((), (), s32[]{:S(2)}) async-start(), calls=%async_computation.28 | async-start | bytes 1966080 | tf_op jit(solution)/shard_map/all_gather | solution.py:40
  504.8 89.3 %reduce-scatter.21.cloned.1.call-start = ((), (), s32[]{:S(2)}) async-start(), calls=%async_computation.25 | async-start | bytes 3932160 | tf_op jit(solution)/shard_map/reduce_scatter | solution.py:44
  528.7 11.5 copy-start.55
  544.6 89.3 %reduce-scatter.25.cloned.1.call-start = ((), (), s32[]{:S(2)}) async-start(), calls=%async_computation.29 | async-start | bytes 3932160 | tf_op jit(solution)/shard_map/reduce_scatter | solution.py:44
  554.4 11.5 copy-start.56
  570.3 94.8 %all-gather.35.cloned.1.call-start = ((), (), s32[]{:S(2)}) async-start(), calls=%async_computation.30 | async-start | bytes 1966080 | tf_op jit(solution)/shard_map/all_gather | solution.py:40
  640.7 61.9 %all-gather.31.cloned.1.call-start = ((), (), s32[]{:S(2)}) async-start(), calls=%async_computation.26 | async-start | bytes 1966080 | tf_op jit(solution)/shard_map/all_gather | solution.py:40
  640.8 24.3 %copy-start.17 = (bf16[1024,512]{1,0:T(8,128)(2,1)S(1)}, bf16[1024,512]{1,0:T(8,128)(2,1)}, u32[]{:S(2)}) copy-start(bf16[1024,512]{1,0:T(8,128)(2,1)} %all-gather.17.cloned.1.call-done) | copy-start | bytes 3145732
  645.0 25.3 %copy-start.21 = (bf16[2,320,1,512]{1,3,0,2:T(8,128)(2,1)S(1)}, bf16[2,320,1,512]{1,3,0,2:T(8,128)(2,1)}, u32[]{:S(2)}) copy-start(bf16[2,320,1,512]{1,3,0,2:T(8,128)(2,1)} %copy-done.20) | copy-start | bytes 1966084
  645.0 177.4 %reduce-scatter.27.cloned.1.call-start = ((), (), s32[]{:S(2)}) async-start(), calls=%async_computation.31 | async-start | bytes 3932160 | tf_op jit(solution)/shard_map/reduce_scatter | solution.py:44
  670.3 7.2 slice-start
  670.3 7.2 slice-start.1
  696.1 6.4 copy-start.38
  702.3 120.2 %reduce-scatter.23.cloned.1.call-start = ((), (), s32[]{:S(2)}) async-start(), calls=%async_computation.27 | async-start | bytes 3932160 | tf_op jit(solution)/shard_map/reduce_scatter | solution.py:44
  705.1 6.5 copy-start.19
  716.8 6.6 copy-start.9
  729.1 6.4 copy-start.31
  735.5 133.1 %reduce-scatter.31.cloned.1.call-start = ((), (), s32[]{:S(2)}) async-start(), calls=%async_computation.33 | async-start | bytes 2228224 | tf_op jit(solution)/shard_map/reduce_scatter | solution.py:232
  740.4 214.7 %reduce-scatter.33.cloned.1.call-start = ((), (), s32[]{:S(2)}) async-start(), calls=%async_computation.34 | async-start | bytes 8912896 | tf_op jit(solution)/shard_map/reduce_scatter | solution.py:233
  752.6 312.1 %reduce-scatter.35.cloned.1.call-start = ((), (), s32[]{:S(2)}) async-start(), calls=%async_computation.35 | async-start | bytes 8912896 | tf_op jit(solution)/shard_map/reduce_scatter | solution.py:234
  765.4 389.2 %reduce-scatter.29.cloned.1.call-start = ((), (), s32[]{:S(2)}) async-start(), calls=%async_computation.32 | async-start | bytes 6684672 | tf_op jit(solution)/shard_map/reduce_scatter | solution.py:231
  775.7 44.4 %copy-start.52 = (f32[1024]{0:T(1024)S(1)}, f32[1024]{0:T(1024)}, u32[]{:S(2)}) copy-start(f32[1024]{0:T(1024)} %get-tuple-element.31) | copy-start | bytes 12292
  775.7 44.4 %copy-start.28 = (bf16[2,160,1024]{2,1,0:T(8,128)(2,1)S(1)}, bf16[2,160,1024]{2,1,0:T(8,128)(2,1)}, u32[]{:S(2)}) copy-start(bf16[2,160,1024]{2,1,0:T(8,128)(2,1)} %get-tuple-element.59) | copy-start | bytes 1966084
  775.7 46.7 %copy-start.2 = (bf16[4,160,1024]{2,1,0:T(8,128)(2,1)S(1)}, bf16[4,160,1024]{2,1,0:T(8,128)(2,1)}, u32[]{:S(2)}) copy-start(bf16[4,160,1024]{2,1,0:T(8,128)(2,1)} %param.9) | copy-start | bytes 3932164
  775.7 46.7 %copy-start.42 = (f32[1024]{0:T(1024)S(1)}, f32[1024]{0:T(1024)}, u32[]{:S(2)}) copy-start(f32[1024]{0:T(1024)} %copy-done.41) | copy-start | bytes 12292
  775.7 46.7 %copy-start.44 = (f32[2,160]{1,0:T(2,128)S(1)}, f32[2,160]{1,0:T(2,128)}, u32[]{:S(2)}) copy-start(f32[2,160]{1,0:T(2,128)} %copy-done.43) | copy-start | bytes 3844
  775.8 46.7 %copy-start.46 = (f32[2,160]{1,0:T(2,128)S(1)}, f32[2,160]{1,0:T(2,128)}, u32[]{:S(2)}) copy-start(f32[2,160]{1,0:T(2,128)} %copy-done.45) | copy-start | bytes 3844
  775.8 46.7 %copy-start.49 = (f32[2,160]{1,0:T(2,128)S(1)}, f32[2,160]{1,0:T(2,128)}, u32[]{:S(2)}) copy-start(f32[2,160]{1,0:T(2,128)} %copy-done.48) | copy-start | bytes 3844
  775.8 46.7 %copy-start.51 = (f32[2,160]{1,0:T(2,128)S(1)}, f32[2,160]{1,0:T(2,128)}, u32[]{:S(2)}) copy-start(f32[2,160]{1,0:T(2,128)} %copy-done.50) | copy-start | bytes 3844
  775.8 88.1 %copy-start.15 = (f32[2,160,1024]{2,1,0:T(8,128)S(1)}, f32[2,160,1024]{2,1,0:T(8,128)}, u32[]{:S(2)}) copy-start(f32[2,160,1024]{2,1,0:T(8,128)} %get-tuple-element.45) | copy-start | bytes 3932164
  (42 other events, 144.6 us)
Sparse Core Ops, SparseCore 0:
  52.2 21.4 all-gather.12
  76.0 45.2 all-gather.14
  123.4 36.7 all-gather.16
  161.6 23.1 all-gather.24
  187.4 37.5 reduce-scatter.12
  227.2 37.5 reduce-scatter.16
  267.0 50.5 all-gather.20
  319.7 22.7 all-gather.18
  344.7 50.7 all-gather.22
  396.8 22.7 all-gather.26
  421.9 38.1 reduce-scatter.14
  462.2 38.3 reduce-scatter.18
  504.4 24.2 all-gather.28
  530.1 24.2 all-gather.32
  556.5 37.5 reduce-scatter.20
  596.3 37.5 reduce-scatter.24
  640.8 24.2 all-gather.34
  666.5 24.2 all-gather.30
  702.4 37.4 reduce-scatter.26
  742.1 37.5 reduce-scatter.22
  784.0 62.3 reduce-scatter.30
  851.6 103.4 reduce-scatter.32
  960.3 104.3 reduce-scatter.34
  1069.5 84.9 reduce-scatter.28
where the time goes:
time: 1170 us; the launch traced here: 1160 us
  waiting for transfers between devices  714 us (61%)
  matrix products  166 us (14%)
  blocking collectives  152 us (13%)
  other arithmetic  74.9 us (6%)
  local copies, waits for them, and re-layouts  30.3 us (3%)
  between operations  22.3 us (2%)
    reduce_scatter x1, waiting for transfers between devices, per_device(): lax.psum_scatter(summed[5], 'dp', scatter_dimension=0, tiled=True)  110 us
    reduce_scatter x1, waiting for transfers between devices, per_device(): lax.psum_scatter(summed[2], 'dp', scatter_dimension=0, tiled=True)  89.9 us
    reduce_scatter x1, waiting for transfers between devices, per_device(): lax.psum_scatter(summed[4], 'dp', scatter_dimension=0, tiled=True)  86.5 us
    all_gather x4, waiting for transfers between devices, full_rows(): return lax.all_gather(piece, 'mp', axis=1, tiled=True)  81.3 us
    reduce_scatter x4, waiting for transfers between devices, row_sums(): return lax.psum_scatter(partial_rows, 'mp', scatter_dimension=1, tiled=True)  76.2 us
    unnamed x2, blocking collectives  67.9 us
    reduce_scatter x4, waiting for transfers between devices, sum_grads(): return lax.psum_scatter(partial_rows, 'mp', scatter_dimension=1, tiled=True)  63.1 us
    all_gather x4, waiting for transfers between devices, full_grads(): return lax.all_gather(piece, 'mp', axis=1, tiled=True)  53.4 us
  transfers between devices with their start and end apart: 24, of which 19 were waited for; matrix products, arithmetic and copies ran while one was open for 20% of the time, Pallas kernels for 0%

commit v1 on v0

v1 whole, which is shorter than its diff:
```python
import functools
import jax
import jax.numpy as jnp
from jax import lax
from jax.experimental import pallas as pl
from jax.experimental.pallas import tpu as pltpu
from jax.sharding import PartitionSpec as P

MESH = pl.DeviceIdType.MESH
HDIM = 64
CW = 256
EPS = 1e-06
F32 = jnp.float32
BF = jnp.bfloat16
L1, L3, L4, L5 = 2, 1, 1, 1
RDY = L3 + L4 + L5
NT = (((1,), (1,)), ((), ()))
NN = (((1,), (0,)), ((), ()))


def dot(a, b, dims=NN):
    return lax.dot_general(a, b, dims, preferred_element_type=F32)


class Place:
    def __init__(self, groups):
        self.groups = groups
        dp = lax.axis_index("dp")
        self.x = lax.axis_index("mp")
        self.c = lax.rem(dp, 2)
        self.y = lax.rem(dp // 2, 2)
        self.z = dp // 4

    def at(self, z, y, c, x):
        return {"dp": (z * 2 + y) * 2 + c, "mp": x}

    def far(self, j):
        return self.at(lax.rem(self.z + j, self.groups), self.y, self.c, self.x)

    def over_x(self):
        return self.at(self.z, self.y, self.c, 1 - self.x)

    def over_y(self):
        return self.at(self.z, 1 - self.y, self.c, self.x)

    def over_c(self):
        return self.at(self.z, self.y, 1 - self.c, self.x)

    def partners(self):
        return [self.far(j) for j in range(1, self.groups)] + [
            self.over_x(), self.over_y(), self.over_c()
        ]


def meet(place):
    barrier = pltpu.get_barrier_semaphore()
    partners = place.partners()
    for partner in partners:
        pl.semaphore_signal(barrier, 1, device_id=partner, device_id_type=MESH)
    pl.semaphore_wait(barrier, len(partners))


def both_first(k):
    return (k < 5) | (lax.rem(k, 4) == 1)


def when(cond, body):
    if isinstance(cond, bool):
        if cond:
            body()
    else:
        pl.when(cond)(body)


def fwd_kernel(cfg, xin, tin, wq, wo, wu, wd, small, krow, kcol, *refs):
    (wg_o, at_o, proj_o, lse_o, o_o, h_o, bnt_o, g_o, gp_o, gy_o, gm_o, gmt_o, out_o, xs_o, ts_o, sm_o, loss_o,
     wg, xs, ts, sm, a, proj, o, lse, h, bn, g, gp, zb, y, tb,
     local_sem, send_sem, recv_sem, extra_send, extra_recv, out_sem, misc_sem) = refs
    H, R = cfg["groups"], cfg["rows"]
    NQ, NO, NF = cfg["nq"], cfg["no"], cfg["nf"]
    NCH = NQ + NO + 2 * NF
    IMG, SEQ, D = xs.shape
    HALF = SEQ // 2
    TOK = IMG * SEQ
    FH = wq.shape[1] // 3
    GRP = NQ // 3
    place = Place(H)
    x, yy, z, c = place.x, place.y, place.z, place.c
    scale = HDIM ** (-0.5)

    def remote(ref, k, i, device):
        return pltpu.make_async_remote_copy(
            ref, ref, send_sem.at[k, i], recv_sem.at[k, i], device_id=device, device_id_type=MESH
        )

    def source(k):
        if k < NQ:
            return wq.at[:, pl.ds((k % 3) * FH + (k // 3) * CW, CW)]
        if k < NQ + NO:
            return wo.at[:, pl.ds(CW * (k - NQ), CW)]
        if k < NQ + NO + NF:
            return wu.at[:, pl.ds(CW * (k - NQ - NO), CW)]
        return wd.at[:, pl.ds(CW * (k - NQ - NO - NF), CW)]

    def own(k):
        return pltpu.make_async_copy(source(k), wg.at[k, x, z, yy, c], local_sem.at[k])

    def own_wait(k):
        pltpu.make_async_copy(wq.at[:, pl.ds(0, CW)], wg.at[k, x, z, yy, c], local_sem.at[k]).wait()

    def relay(k):
        first = jnp.where(both_first(k), 1, 1 - c)
        xa = jnp.where(first == 1, 1 - x, x)
        ya = jnp.where(first == 1, yy, 1 - yy)
        return xa, ya, jnp.where(first == 1, x, 1 - x), jnp.where(first == 1, 1 - yy, yy)

    def s1(k):
        own_wait(k)
        for j in range(1, H):
            remote(wg.at[k, x, z, yy, c], k, j - 1, place.far(j)).start()

    def s2(k):
        for j in range(1, H):
            remote(wg.at[k, x, lax.rem(z + H - j, H), yy, c], k, j - 1, place.far(j)).wait_recv()
        xa, ya, xb, yb = relay(k)
        remote(wg.at[k, x, :, yy, c], k, H - 1, place.at(z, ya, c, xa)).start()
        remote(wg.at[k, x, :, yy, c], k, H, place.at(z, yb, c, xb)).start()

    def s3(k):
        xa, ya, xb, yb = relay(k)
        remote(wg.at[k, xa, :, ya, c], k, H - 1, place.at(z, ya, c, xa)).wait_recv()
        remote(wg.at[k, xa, :, ya, c], k, H + 1, place.at(z, yb, c, xb)).start()

    def s4(k):
        xa, ya, xb, yb = relay(k)
        remote(wg.at[k, xb, :, yb, c], k, H, place.at(z, yb, c, xb)).wait_recv()
        remote(wg.at[k, 1 - x, :, 1 - yy, c], k, H + 1, place.at(z, yb, c, xb)).wait_recv()
        remote(wg.at[k, :, :, :, c], k, H + 2, place.over_c()).start()

    def keep_chunk(k):
        return pltpu.make_async_copy(wg.at[k], wg_o.at[k], out_sem.at[k])

    def s5(k):
        remote(wg.at[k, :, :, :, 1 - c], k, H + 2, place.over_c()).wait_recv()
        keep_chunk(k).start()

    def step(t):
        def inside(k):
            return (0 <= k < NCH) if isinstance(k, int) else (k >= 0) & (k < NCH)

        when(inside(t + L1), lambda: s1(t + L1))
        when(inside(t), lambda: s2(t))
        when(inside(t - L3), lambda: s3(t - L3))
        when(inside(t - L3 - L4), lambda: s4(t - L3 - L4))
        when(inside(t - RDY), lambda: s5(t - RDY))

    kept = []

    def keep(src, dst):
        copy = pltpu.make_async_copy(src, dst, misc_sem.at[len(kept)])
        copy.start()
        kept.append(copy)

    def extra(src, dst, i, device):
        return pltpu.make_async_remote_copy(
            src, dst, extra_send.at[i], extra_recv.at[i], device_id=device, device_id_type=MESH
        )

    for k in range(NCH):
        own(k).start()
    mine = pl.ds(HALF * x, HALF)
    xl = pltpu.make_async_copy(xin.at[pl.ds(IMG * x, IMG)], xs.at[:, mine], misc_sem.at[30])
    tl = pltpu.make_async_copy(tin.at[pl.ds(IMG * x, IMG)], ts.at[:, mine], misc_sem.at[31])
    sl = pltpu.make_async_copy(small, sm.at[z, yy, c], misc_sem.at[29])
    xl.start()
    tl.start()
    sl.start()
    meet(place)
    xr = extra(xin.at[pl.ds(IMG * (1 - x), IMG)], xs.at[:, mine], 0, place.over_x())
    tr = extra(tin.at[pl.ds(IMG * (1 - x), IMG)], ts.at[:, mine], 1, place.over_x())
    sl.wait()
    for j in range(1, H):
        extra(sm.at[z, yy, c], sm.at[z, yy, c], 3 + j, place.far(j)).start()
    for k in range(L1):
        s1(k)
    xr.start()
    for j in range(1, H):
        extra(sm.at[z, yy, c], sm.at[lax.rem(z + H - j, H), yy, c], 3 + j, place.far(j)).wait_recv()
    extra(sm.at[:, yy, c], sm.at[:, yy, c], 2, place.over_y()).start()
    step(0)
    extra(sm.at[:, 1 - yy, c], sm.at[:, 1 - yy, c], 2, place.over_y()).wait_recv()
    extra(sm.at[:, :, c], sm.at[:, :, c], 3, place.over_c()).start()
    step(1)
    extra(sm.at[:, :, 1 - c], sm.at[:, :, 1 - c], 3, place.over_c()).wait_recv()
    totals = jnp.sum(sm[...].reshape(H * 4, 8, D), axis=0)
    sm_o[...] = totals
    xl.wait()
    extra(xin.at[pl.ds(IMG * (1 - x), IMG)], xs.at[:, pl.ds(HALF * (1 - x), HALF)], 0, place.over_x()).wait_recv()
    keep(xs, xs_o)

    RB = 32

    def rows_of(ref, r):
        per = SEQ // RB
        return ref[r // per, pl.ds(pl.multiple_of(lax.rem(r, per) * RB, RB), RB)]

    def norm_to(values, gain):
        centre = values - jnp.mean(values, axis=-1, keepdims=True)
        spread = jnp.mean(centre * centre, axis=-1, keepdims=True)
        return (centre * lax.rsqrt(spread + EPS) * gain).astype(BF)

    @pl.loop(0, TOK // RB)
    def _(r):
        a[pl.ds(pl.multiple_of(r * RB, RB), RB)] = norm_to(rows_of(xs, r).astype(F32), sm_o[0:1])

    def transposed(src, dst):
        @pl.loop(0, D // 128)
        def _(d):
            t = jnp.transpose(src[:, pl.ds(pl.multiple_of(d * 128, 128), 128)].astype(F32))
            t = t.reshape(64 // R, 2, R, TOK)
            for p in range(2):
                dst[p, pl.ds(pl.multiple_of(d * 64, 64), 64)] = t[:, p].reshape(64, TOK).astype(BF)

    step(2)
    transposed(a, tb)
    keep(tb, at_o)

    def chunk(k, half):
        return wg[k, half].reshape(D, CW)

    def project(k):
        @pl.loop(0, 2)
        def _(half):
            proj[k, half] = dot(a[...], chunk(k, half)).astype(BF).reshape(IMG, SEQ, CW)

    lane = lax.broadcasted_iota(jnp.int32, (SEQ, CW), 1) // HDIM

    def attend(group, u):
        half, i = u // IMG, lax.rem(u, IMG)
        q = proj[3 * group, half, i]
        key = proj[3 * group + 1, half, i]
        val = proj[3 * group + 2, half, i]
        allowed = krow[IMG * x + i, 0:1] > 0
        total = jnp.zeros((SEQ, CW), F32)
        logs = jnp.zeros((SEQ, 128), F32)
        spot = lax.broadcasted_iota(jnp.int32, (SEQ, 128), 1)
        for head in range(CW // HDIM):
            scores = dot(jnp.where(lane == head, q, 0), key, NT) * scale
            scores = jnp.where(allowed, scores, -1e30)
            top = jnp.max(scores, axis=-1, keepdims=True)
            raised = jnp.exp(scores - top)
            norm = jnp.sum(raised, axis=-1, keepdims=True)
            soft = (raised / norm).astype(BF)
            total = total + dot(soft, jnp.where(lane == head, val, 0))
            logs = jnp.where(spot == head, top + jnp.log(norm), logs)
        o[group, half, i] = total.astype(BF)
        lse[group, half, i] = logs

    for k in range(3):
        step(k + RDY)
        project(k)
    done = 3 + RDY
    for group in range(GRP):
        if group:
            for k in range(3 * group, 3 * group + 3):
                while done <= k + RDY:
                    step(done)
                    done += 1
                project(k)

        @pl.loop(0, 2 * IMG)
        def _(u, group=group, done=done):
            pl.when(lax.rem(u, 2) == 0)(lambda: step(done + u // 2))
            attend(group, u)
        done += IMG
    keep(proj, proj_o)
    keep(lse, lse_o)
    keep(o, o_o)
    while done <= NQ + NO - 1 + RDY:
        step(done)
        done += 1

    def gathered(src, k, half):
        return src[k, half].reshape(TOK, CW)

    for k in range(NO):
        for half in range(2):
            part = dot(gathered(o, k, half), chunk(NQ + k, half), NT)
            if k == 0 and half == 0:
                h[...] = xs[...].reshape(TOK, D).astype(F32) + part
            else:
                h[...] += part
    keep(h, h_o)

    @pl.loop(0, TOK // RB)
    def _(r):
        at = pl.ds(pl.multiple_of(r * RB, RB), RB)
        bn[at] = norm_to(h[at], sm_o[1:2])

    tr.start()
    first_up = NQ + NO

    def gelu(k, half):
        GB = 64

        @pl.loop(0, TOK // GB)
        def _(r):
            at = pl.ds(pl.multiple_of(r * GB, GB), GB)
            v = zb[at]
            cdf = 0.5 * (1.0 + lax.erf(v * 0.7071067811865476))
            g[k, half, at] = (v * cdf).astype(BF)
            gp[k, half, at] = (cdf + v * (jnp.exp(-0.5 * (v * v)) * 0.3989422804014327)).astype(BF)

    @pl.loop(0, NF)
    def _(k):
        step(done + k)

        @pl.loop(0, 2)
        def _(half):
            zb[...] = dot(bn[...], chunk(first_up + k, half))
            gelu(k, half)
    done += NF
    keep(g, g_o)
    keep(gp, gp_o)
    first_down = first_up + NF
    kept[1].wait()
    transposed(bn, tb)
    keep(tb, bnt_o)
    y[...] = h[...]

    @pl.loop(0, NF)
    def _(k):
        step(done + k)

        @pl.loop(0, 2)
        def _(half):
            y[...] += dot(g[k, half], chunk(first_down + k, half), NT)

    tl.wait()
    extra(tin.at[pl.ds(IMG * (1 - x), IMG)], ts.at[:, pl.ds(HALF * (1 - x), HALF)], 1, place.over_x()).wait_recv()
    keep(ts, ts_o)
    loss_o[...] = jnp.zeros_like(loss_o)
    factor = 2.0 * cfg["tokens"] / sm_o[2:3]
    xs_ref = xs

    for copy in kept[:1]:
        copy.wait()

    @pl.loop(0, TOK // RB)
    def _(r):
        at = pl.ds(pl.multiple_of(r * RB, RB), RB)
        per = SEQ // RB
        img, pos = r // per, pl.multiple_of(lax.rem(r, per) * RB, RB)
        res = y[at]
        kept_rows = jnp.tile(kcol[IMG * x + img, pl.ds(pos, RB)], (1, D // 128))
        xs_ref[img, pl.ds(pos, RB)] = (res * kept_rows).astype(BF)
        error = res - ts[img, pl.ds(pos, RB)].astype(F32)
        per_row = jnp.mean(error * error, axis=-1, keepdims=True) * kept_rows[:, :1]
        loss_o[...] += jnp.sum(per_row)
        grad = factor * kept_rows * error
        y[at] = grad
        a[at] = grad.astype(BF)

    keep(xs, out_o)
    keep(y, gy_o)
    keep(a, gm_o)
    kept[8].wait()
    transposed(a, tb)
    keep(tb, gmt_o)
    for n, copy in enumerate(kept):
        if n not in (0, 1, 8):
            copy.wait()
    xr.wait_send()
    tr.wait_send()
    for j in range(1, H):
        extra(sm.at[z, yy, c], sm.at[z, yy, c], 3 + j, place.far(j)).wait_send()
    extra(sm.at[:, yy, c], sm.at[:, yy, c], 2, place.over_y()).wait_send()
    extra(sm.at[:, :, c], sm.at[:, :, c], 3, place.over_c()).wait_send()

    @pl.loop(0, NCH)
    def _(k):
        keep_chunk(k).wait()
        for j in range(1, H):
            remote(wg.at[k, x, z, yy, c], k, j - 1, place.far(j)).wait_send()
        for i in (H - 1, H, H + 1):
            remote(wg.at[k, x, :, yy, c], k, i, place.over_x()).wait_send()
        remote(wg.at[k, :, :, :, c], k, H + 2, place.over_c()).wait_send()


def any_spec():
    return pl.BlockSpec(memory_space=pl.ANY)


def vmem_spec():
    return pl.BlockSpec(memory_space=pltpu.VMEM)


def forward(cfg, xin, tin, wq, wo, wu, wd, small, krow, kcol):
    H, R = cfg["groups"], cfg["rows"]
    NQ, NO, NF = cfg["nq"], cfg["no"], cfg["nf"]
    NCH = NQ + NO + 2 * NF
    IMG = xin.shape[0] // 2
    SEQ, D = 2 * xin.shape[1], xin.shape[2]
    TOK = IMG * SEQ
    GRP = NQ // 3
    wg = (NCH, 2, H, 2, 2, R, CW)
    lhs = (2, D // 2, TOK)
    big = (NF, 2, TOK, CW)
    shapes = [
        (wg, BF), (lhs, BF), ((NQ, 2, IMG, SEQ, CW), BF), ((GRP, 2, IMG, SEQ, 128), F32),
        ((GRP, 2, IMG, SEQ, CW), BF), ((TOK, D), F32), (lhs, BF), (big, BF), (big, BF),
        ((TOK, D), F32), ((TOK, D), BF), (lhs, BF), ((IMG, SEQ, D), BF), ((IMG, SEQ, D), BF), ((IMG, SEQ, D), BF),
        ((8, D), F32), ((8, 128), F32),
    ]
    return pl.pallas_call(
        functools.partial(fwd_kernel, cfg),
        name="gather_forward",
        out_shape=[jax.ShapeDtypeStruct(s, t) for s, t in shapes],
        in_specs=[any_spec()] * 7 + [vmem_spec()] * 2,
        out_specs=[any_spec()] * 15 + [vmem_spec()] * 2,
        scratch_shapes=[
            pltpu.VMEM(wg, BF), pltpu.VMEM((IMG, SEQ, D), BF), pltpu.VMEM((IMG, SEQ, D), BF),
            pltpu.VMEM((H, 2, 2, 8, D), F32), pltpu.VMEM((TOK, D), BF),
            pltpu.VMEM((NQ, 2, IMG, SEQ, CW), BF), pltpu.VMEM((GRP, 2, IMG, SEQ, CW), BF),
            pltpu.VMEM((GRP, 2, IMG, SEQ, 128), F32), pltpu.VMEM((TOK, D), F32), pltpu.VMEM((TOK, D), BF),
            pltpu.VMEM(big, BF), pltpu.VMEM(big, BF), pltpu.VMEM((TOK, CW), F32), pltpu.VMEM((TOK, D), F32),
            pltpu.VMEM(lhs, BF),
            pltpu.SemaphoreType.DMA((NCH,)), pltpu.SemaphoreType.DMA((NCH, H + 3)),
            pltpu.SemaphoreType.DMA((NCH, H + 3)), pltpu.SemaphoreType.DMA((H + 4,)),
            pltpu.SemaphoreType.DMA((H + 4,)), pltpu.SemaphoreType.DMA((NCH,)), pltpu.SemaphoreType.DMA((32,)),
        ],
        compiler_params=pltpu.CompilerParams(
            collective_id=0, has_side_effects=True, vmem_limit_bytes=63 * 2**20
        ),
    )(xin, tin, wq, wo, wu, wd, small, krow, kcol)


def config(inputs, weights):
    rows = weights[0].shape[0]
    dps = lax.axis_size("dp")
    return {
        "groups": dps // 4,
        "rows": rows,
        "nq": weights[0].shape[1] * weights[0].shape[2] // CW,
        "no": weights[1].shape[1] // CW,
        "nf": weights[2].shape[1] // CW,
        "tokens": float(inputs.shape[0] * inputs.shape[1] * dps * lax.axis_size("mp")),
    }


def prepare(inputs, keep_mask, gain_attn, gain_mlp):
    R, D = gain_attn.shape[0], inputs.shape[2]
    dps = D // R
    here = lax.broadcasted_iota(jnp.int32, (1, D), 1) // R == lax.axis_index("dp")
    count = jnp.sum(keep_mask).astype(F32)
    small = jnp.concatenate(
        [
            jnp.where(here, jnp.tile(gain_attn.astype(F32), dps)[None], 0.0),
            jnp.where(here, jnp.tile(gain_mlp.astype(F32), dps)[None], 0.0),
            jnp.full((6, D), count, F32),
        ],
        axis=0,
    )
    mask = keep_mask.astype(F32)
    krow = jnp.broadcast_to(mask[:, None, :], (mask.shape[0], 8, mask.shape[1]))
    kcol = jnp.broadcast_to(mask[:, :, None], mask.shape + (128,))
    return small, krow, kcol


SLOTS = 3
WSLOTS = 4
LAGS = (1, 4, 7, 9)


def bwd_kernel(cfg, wg, at_i, proj_i, lse_i, o_i, h_i, bnt_i, g_i, gp_i, gy_i, gm_i, gmt_i, out_i, xs_i,
               totals, loss_i, krow, *refs):
    (out_o, ig_o, dw_o, stat_o,
     q, snd, rcv, near, farr, dw, wb, gb_buf, gpb, gz, zb, gm, lhs1, lhs2, acc, gh, h, o, go, proj, lse, xb, stat, sbuf,
     core_send, core_recv, credit, near_send, near_recv, far_send, far_recv, extra_send, extra_recv,
     wsem, gsem, misc_sem, dw_sem) = refs
    H, R = cfg["groups"], cfg["rows"]
    NQ, NO, NF = cfg["nq"], cfg["no"], cfg["nf"]
    NCH = NQ + NO + 2 * NF
    IMG, SEQ, D = xb.shape
    HALF = SEQ // 2
    TOK = IMG * SEQ
    GRP = NQ // 3
    place = Place(H)
    x, yy, z, c = place.x, place.y, place.z, place.c
    scale = HDIM ** (-0.5)

    def ident(p):
        ff = jnp.where(lax.rem(p, 2) == 0, NQ + NO + NF + p // 2, NQ + NO + p // 2)
        return jnp.where(p < 2 * NF, ff, jnp.where(p < 2 * NF + NO, p - 2 * NF + NQ, p - 2 * NF - NO))

    def relay(k):
        first = jnp.where(both_first(k), 1, 1 - c)
        xa = jnp.where(first == 1, 1 - x, x)
        ya = jnp.where(first == 1, yy, 1 - yy)
        return xa, ya, jnp.where(first == 1, x, 1 - x), jnp.where(first == 1, 1 - yy, yy)

    loads = []

    def load(src, dst):
        copy = pltpu.make_async_copy(src, dst, misc_sem.at[len(loads)])
        copy.start()
        loads.append(copy)
        return copy

    def wload(n):
        return pltpu.make_async_copy(wg.at[ident(n)], wb.at[lax.rem(n, WSLOTS)], wsem.at[n])

    def gload(j):
        s = lax.rem(j, 2)
        return (pltpu.make_async_copy(g_i.at[j], gb_buf.at[s], gsem.at[j, 0]),
                pltpu.make_async_copy(gp_i.at[j], gpb.at[s], gsem.at[j, 1]))

    gm_l = load(gm_i, gm)
    gmt_l = load(gmt_i, lhs1)
    for j in range(2):
        for copy in gload(jnp.int32(j)):
            copy.start()
    for n in range(WSLOTS):
        wload(jnp.int32(n)).start()
    bnt_l = load(bnt_i, lhs2)
    out_l = load(out_i, xb)
    gy_l = load(gy_i, gh)
    h_l = load(h_i, h)
    o_l = load(o_i, o)
    proj_l = load(proj_i, proj)
    lse_l = load(lse_i, lse)

    def extra(src, dst, i, device):
        return pltpu.make_async_remote_copy(
            src, dst, extra_send.at[i], extra_recv.at[i], device_id=device, device_id_type=MESH
        )

    meet(place)

    def core_copy(p, start=False):
        s = lax.rem(p, SLOTS)
        return pltpu.make_async_remote_copy(
            snd.at[s], rcv.at[s], core_send.at[p], core_recv.at[p], device_id=place.over_c(), device_id_type=MESH
        )

    def near_copy(src, k, i, device):
        return pltpu.make_async_remote_copy(
            src, near.at[k, i], near_send.at[k, i], near_recv.at[k, i], device_id=device, device_id_type=MESH
        )

    def far_copy(k, zd, j):
        return pltpu.make_async_remote_copy(
            q.at[k, x, zd, yy], farr.at[k, j - 1], far_send.at[k, j - 1], far_recv.at[k, j - 1],
            device_id=place.far(j), device_id_type=MESH
        )

    def produce(p, lhs, rhs):
        k = ident(p)
        s = lax.rem(p, SLOTS)
        pl.when(p >= SLOTS)(lambda: core_copy(p - SLOTS).wait_send())

        @pl.loop(0, 2)
        def _(half):
            snd[s, half] = dot(lhs[1 - c], rhs(half)).astype(BF).reshape(H, 2, R, CW)
            q[k, half] = dot(lhs[c], rhs(half)).astype(BF).reshape(H, 2, R, CW)

        pl.when(p >= SLOTS)(lambda: pl.semaphore_wait(credit, 1))
        core_copy(p).start()

    def added(k, xi, yi, others):
        @pl.loop(0, H)
        def _(n):
            total = q[k, xi, n, yi].astype(F32)
            for other in others:
                total = total + near[k, other, n].astype(F32)
            q[k, xi, n, yi] = total.astype(BF)

    def r1(p):
        k = ident(p)
        s = lax.rem(p, SLOTS)
        core_copy(p).wait_recv()

        @pl.loop(0, 2 * H)
        def _(n):
            i, m = n // H, lax.rem(n, H)
            for y2 in range(2):
                q[k, i, m, y2] = (q[k, i, m, y2].astype(F32) + rcv[s, i, m, y2].astype(F32)).astype(BF)

        pl.when(p + SLOTS < NCH)(
            lambda: pl.semaphore_signal(credit, 1, device_id=place.over_c(), device_id_type=MESH)
        )
        xa, ya, xo, yo = relay(k)
        near_copy(q.at[k, 1 - x, :, 1 - yy], k, 0, place.at(z, yo, c, xo)).start()
        near_copy(q.at[k, xo, :, yo], k, 1, place.at(z, yo, c, xo)).start()

    def r2(p):
        k = ident(p)
        xa, ya, xo, yo = relay(k)
        near_copy(q.at[k, 1 - x, :, 1 - yy], k, 0, place.at(z, yo, c, xo)).wait_recv()
        added(k, xa, ya, (0,))
        near_copy(q.at[k, xa, :, ya], k, 2, place.at(z, ya, c, xa)).start()

    def r3(p):
        k = ident(p)
        xa, ya, xo, yo = relay(k)
        near_copy(q.at[k, xo, :, yo], k, 1, place.at(z, yo, c, xo)).wait_recv()
        near_copy(q.at[k, xa, :, ya], k, 2, place.at(z, ya, c, xa)).wait_recv()
        added(k, x, yy, (1, 2))
        for j in range(1, H):
            far_copy(k, lax.rem(z + j, H), j).start()

    def dw_copy(k):
        return pltpu.make_async_copy(dw.at[k], dw_o.at[k], dw_sem.at[k])

    def r4(p):
        k = ident(p)
        total = q[k, x, z, yy].astype(F32)
        for j in range(1, H):
            far_copy(k, lax.rem(z + j, H), j).wait_recv()
            total = total + farr[k, j - 1].astype(F32)
        dw[k] = total
        dw_copy(k).start()

    stages = (r1, r2, r3, r4)

    def tick(p, lags=LAGS):
        for stage, lag in zip(stages, lags):
            n = p - lag
            if isinstance(n, int):
                if 0 <= n < NCH:
                    stage(jnp.int32(n))
            else:
                pl.when((n >= 0) & (n < NCH))(lambda stage=stage, n=n: stage(n))

    gm_l.wait()
    gmt_l.wait()
    bnt_l.wait()

    def wchunk(n, half):
        return wb[lax.rem(n, WSLOTS), half].reshape(D, CW)

    def wnext(n):
        pl.when(n + WSLOTS < NCH)(lambda: wload(n + WSLOTS).start())

    GB = 64
    acc[...] = jnp.zeros_like(acc)

    @pl.loop(0, NF)
    def _(j):
        s = lax.rem(j, 2)
        gl, gpl = gload(j)
        gl.wait()
        produce(2 * j, lhs1, lambda half: gb_buf[s, half])
        gpl.wait()
        wload(2 * j).wait()
        tick(2 * j)

        @pl.loop(0, 2)
        def _(half):
            zb[...] = dot(gm[...], wchunk(2 * j, half))

            @pl.loop(0, TOK // GB)
            def _(r):
                at = pl.ds(pl.multiple_of(r * GB, GB), GB)
                gz[half, at] = (zb[at] * gpb[s, half, at].astype(F32)).astype(BF)

        wnext(2 * j)

        @pl.when(j + 2 < NF)
        def _():
            for copy in gload(j + 2):
                copy.start()

        produce(2 * j + 1, lhs2, lambda half: gz[half])
        tick(2 * j + 1)
        wload(2 * j + 1).wait()

        @pl.loop(0, 2)
        def _(half):
            acc[...] += dot(gz[half], wchunk(2 * j + 1, half), NT)

        wnext(2 * j + 1)

    mine, other = pl.ds(HALF * x, HALF), pl.ds(HALF * (1 - x), HALF)
    out_l.wait()
    out_r = extra(xb.at[:, other], out_o.at[pl.ds(IMG * x, IMG)], 0, place.over_x())
    out_r.start()
    out_c = pltpu.make_async_copy(xb.at[:, mine], out_o.at[pl.ds(IMG * x, IMG)], misc_sem.at[30])
    out_c.start()

    RB = 32

    def norm_back(values, grad, gain):
        centre = values - jnp.mean(values, axis=-1, keepdims=True)
        spread = jnp.mean(centre * centre, axis=-1, keepdims=True)
        scaled = lax.rsqrt(spread + EPS)
        unit = centre * scaled
        e = grad * gain
        first = jnp.mean(e, axis=-1, keepdims=True)
        second = jnp.mean(e * unit, axis=-1, keepdims=True)
        return scaled * (e - first - unit * second), grad * unit

    def fold(v):
        return jnp.sum(v.reshape(RB // 8, 8, D), axis=0)

    stat[...] = jnp.zeros_like(stat)
    gy_l.wait()
    h_l.wait()

    @pl.loop(0, TOK // RB)
    def _(r):
        at = pl.ds(pl.multiple_of(r * RB, RB), RB)
        back, product = norm_back(h[at], acc[at], totals[1:2])
        total = gh[at] + back
        gh[at] = total
        gm[at] = total.astype(BF)
        stat[1] += fold(product)

    def transposed(src, dst):
        @pl.loop(0, D // 128)
        def _(d):
            t = jnp.transpose(src[:, pl.ds(pl.multiple_of(d * 128, 128), 128)].astype(F32))
            t = t.reshape(64 // R, 2, R, TOK)
            for p in range(2):
                dst[p, pl.ds(pl.multiple_of(d * 64, 64), 64)] = t[:, p].reshape(64, TOK).astype(BF)

    at_l = load(at_i, lhs2)
    transposed(gm, lhs1)
    o_l.wait()
    base = 2 * NF
    for k in range(NO):
        produce(jnp.int32(base + k), lhs1, lambda half, k=k: o[k, half].reshape(TOK, CW))
        tick(base + k)
        wload(jnp.int32(base + k)).wait()

        @pl.loop(0, 2)
        def _(half, k=k):
            go[k, half] = dot(gm[...], wchunk(jnp.int32(base + k), half)).astype(BF).reshape(IMG, SEQ, CW)

        wnext(jnp.int32(base + k))
    proj_l.wait()
    lse_l.wait()
    lane = lax.broadcasted_iota(jnp.int32, (SEQ, CW), 1) // HDIM
    TN = (((0,), (0,)), ((), ()))

    def attend_back(group, u):
        half, i = u // IMG, lax.rem(u, IMG)
        qr, kr, vr = 3 * group, 3 * group + 1, 3 * group + 2
        query, key, val = proj[qr, half, i], proj[kr, half, i], proj[vr, half, i]
        grad = go[group, half, i]
        logs = lse[group, half, i]
        allowed = krow[IMG * x + i, 0:1] > 0
        gq = jnp.zeros((SEQ, CW), F32)
        gk = jnp.zeros((SEQ, CW), F32)
        gv = jnp.zeros((SEQ, CW), F32)
        for head in range(CW // HDIM):
            of_head = lane == head
            qm = jnp.where(of_head, query, 0)
            gom = jnp.where(of_head, grad, 0)
            scores = jnp.where(allowed, dot(qm, key, NT) * scale, -1e30)
            soft = jnp.exp(scores - logs[:, head:head + 1])
            gsoft = dot(gom, val, NT)
            inner = jnp.sum(gsoft * soft, axis=-1, keepdims=True)
            gs = (soft * (gsoft - inner)).astype(BF)
            gq = gq + dot(gs, jnp.where(of_head, key, 0))
            gk = gk + dot(gs, qm, TN)
            gv = gv + dot(soft.astype(BF), gom, TN)
        proj[qr, half, i] = (gq * scale).astype(BF)
        proj[kr, half, i] = (gk * scale).astype(BF)
        proj[vr, half, i] = gv.astype(BF)

    acc[...] = jnp.zeros_like(acc)
    at_l.wait()
    out_c.wait()
    out_r.wait_send()
    xs_l = load(xs_i, xb)
    pos = [base + NO - lag for lag in LAGS]

    def advance(n, upto):
        for i, stage in enumerate(stages):
            for _ in range(n):
                if pos[i] < upto:
                    stage(jnp.int32(pos[i]))
                    pos[i] += 1

    for group in range(GRP):
        for i in range(1):
            advance(1, base + NO + 3 * group)

        @pl.loop(0, 2 * IMG)
        def _(u, group=group):
            attend_back(group, u)

        for k in range(3 * group, 3 * group + 3):
            p = base + NO + k
            produce(jnp.int32(p), lhs2, lambda half, k=k: proj[k, half].reshape(TOK, CW))
            advance(2, p)
            wload(jnp.int32(p)).wait()

            @pl.loop(0, 2)
            def _(half, k=k, p=p):
                acc[...] += dot(proj[k, half].reshape(TOK, CW), wchunk(jnp.int32(p), half), NT)

            wnext(jnp.int32(p))

    xs_l.wait()
    advance(2, NCH)

    @pl.loop(0, TOK // RB)
    def _(r):
        at = pl.ds(pl.multiple_of(r * RB, RB), RB)
        per = SEQ // RB
        img, row = r // per, pl.multiple_of(lax.rem(r, per) * RB, RB)
        back, product = norm_back(xb[img, pl.ds(row, RB)].astype(F32), acc[at], totals[0:1])
        xb[img, pl.ds(row, RB)] = (gh[at] + back).astype(BF)
        stat[0] += fold(product)

    ig_r = extra(xb.at[:, other], ig_o.at[pl.ds(IMG * x, IMG)], 1, place.over_x())
    ig_r.start()
    ig_c = pltpu.make_async_copy(xb.at[:, mine], ig_o.at[pl.ds(IMG * x, IMG)], misc_sem.at[31])
    ig_c.start()

    row = lax.broadcasted_iota(jnp.int32, (8, D), 0)
    small = jnp.where(row == 0, jnp.sum(stat[0], axis=0, keepdims=True),
                      jnp.where(row == 1, jnp.sum(stat[1], axis=0, keepdims=True),
                                jnp.tile(loss_i[...], (1, D // 128))))
    for n, partner in enumerate((place.over_c(), place.over_y(), place.over_x())):
        sbuf[2 * n] = small
        copy = extra(sbuf.at[2 * n], sbuf.at[2 * n + 1], 2 + n, partner)
        copy.start()
        advance(2, NCH)
        copy.wait()
        small = small + sbuf[2 * n + 1]
    stat_o[z] = small
    for j in range(1, H):
        extra(stat_o.at[z], stat_o.at[z], 4 + j, place.far(j)).start()
    while pos[-1] < NCH:
        advance(1, NCH)
    for j in range(1, H):
        copy = extra(stat_o.at[z], stat_o.at[lax.rem(z + H - j, H)], 4 + j, place.far(j))
        copy.wait()

    out_r.wait_recv()
    ig_r.wait()
    ig_c.wait()

    @pl.loop(NCH - SLOTS, NCH)
    def _(p):
        core_copy(p).wait_send()

    @pl.loop(0, NCH)
    def _(k):
        dw_copy(k).wait()
        for i in range(3):
            near_copy(q.at[k, x, :, yy], k, i, place.over_x()).wait_send()
        for j in range(1, H):
            far_copy(k, z, j).wait_send()


def backward(cfg, saved, krow):
    (wg, at, proj, lse, o, h, bnt, g, gp, gy, gm, gmt, out, xs, ts, totals, loss) = saved
    H, R = cfg["groups"], cfg["rows"]
    NQ, NO, NF = cfg["nq"], cfg["no"], cfg["nf"]
    NCH = NQ + NO + 2 * NF
    IMG, SEQ, D = xs.shape
    TOK = IMG * SEQ
    lhs = (2, D // 2, TOK)
    half = (2, H, 2, R, CW)
    vm = pltpu.VMEM
    dma = pltpu.SemaphoreType.DMA
    return pl.pallas_call(
        functools.partial(bwd_kernel, cfg),
        name="backward_reduce",
        out_shape=[
            jax.ShapeDtypeStruct((2 * IMG, SEQ // 2, D), BF), jax.ShapeDtypeStruct((2 * IMG, SEQ // 2, D), BF),
            jax.ShapeDtypeStruct((NCH, R, CW), F32), jax.ShapeDtypeStruct((H, 8, D), F32),
        ],
        in_specs=[any_spec()] * 14 + [vmem_spec()] * 3,
        out_specs=[any_spec()] * 3 + [vmem_spec()],
        scratch_shapes=[
            vm((NCH,) + half, BF), vm((SLOTS,) + half, BF), vm((SLOTS,) + half, BF),
            vm((NCH, 3, H, R, CW), BF), vm((NCH, H - 1, R, CW), BF), vm((NCH, R, CW), F32),
            vm((WSLOTS, 2, H, 2, 2, R, CW), BF), vm((2, 2, TOK, CW), BF), vm((2, 2, TOK, CW), BF),
            vm((2, TOK, CW), BF), vm((TOK, CW), F32), vm((TOK, D), BF), vm(lhs, BF), vm(lhs, BF),
            vm((TOK, D), F32), vm((TOK, D), F32), vm((TOK, D), F32), vm(o.shape, BF), vm(o.shape, BF),
            vm(proj.shape, BF), vm(lse.shape, F32), vm(xs.shape, BF), vm((2, 8, D), F32), vm((6, 8, D), F32),
            dma((NCH,)), dma((NCH,)), pltpu.SemaphoreType.REGULAR, dma((NCH, 3)), dma((NCH, 3)),
            dma((NCH, H - 1)), dma((NCH, H - 1)), dma((H + 4,)), dma((H + 4,)),
            dma((NCH,)), dma((NF, 2)), dma((32,)), dma((NCH,)),
        ],
        compiler_params=pltpu.CompilerParams(
            collective_id=1, has_side_effects=True, vmem_limit_bytes=63 * 2**20
        ),
    )(wg, at, proj, lse, o, h, bnt, g, gp, gy, gm, gmt, out, xs, totals, loss, krow)


def per_device(
    inputs, teacher, keep_mask, gain_attn, qkv_weight, out_weight, gain_mlp, up_weight, down_weight
):
    cfg = config(inputs, (qkv_weight, out_weight, up_weight, down_weight))
    R, NQ, NO, NF = cfg["rows"], cfg["nq"], cfg["no"], cfg["nf"]
    small, krow, kcol = prepare(inputs, keep_mask, gain_attn, gain_mlp)
    saved = forward(
        cfg, inputs, teacher, qkv_weight.reshape(R, -1), out_weight, up_weight, down_weight, small, krow, kcol
    )
    output, grad_in, dw, stats = backward(cfg, saved, krow)
    total = jnp.sum(stats, axis=0)
    start = lax.axis_index("dp") * R
    gains = lax.dynamic_slice(total, (0, start), (2, R))
    loss = total[2, 0] / saved[15][2, 0]
    qkv = dw[:NQ].reshape(NQ // 3, 3, R, CW).transpose(2, 1, 0, 3).reshape(qkv_weight.shape)

    def columns(first, count):
        return dw[first:first + count].transpose(1, 0, 2).reshape(R, count * CW)

    return (
        output,
        loss,
        grad_in.astype(F32),
        gains[0],
        qkv,
        columns(NQ, NO),
        gains[1],
        columns(NQ + NO, NF),
        columns(NQ + NO + NF, NF),
    )


def solution(mesh):
    rows = P("dp", "mp", None)
    weight = P("dp", "mp")
    qkv = P("dp", None, "mp")
    return jax.shard_map(
        per_device,
        mesh=mesh,
        in_specs=(rows, rows, P("dp", None), P("dp"), qkv, weight, P("dp"), weight, weight),
        out_specs=(rows, P(), rows, P("dp"), qkv, weight, P("dp"), weight, weight),
        check_vma=False,
    )
```

time: 1170 us -> 391 us (0.33)
  waiting for transfers between devices: 714 us -> 0 us
  Pallas kernels: 0 us -> 370 us
  matrix products: 166 us -> 0 us
  blocking collectives: 152 us -> 0 us
  other arithmetic: 74.9 us -> 5.37 us
  local copies, waits for them, and re-layouts: 30.3 us -> 11.5 us
  between operations: 22.3 us -> 3.84 us
    reduce_scatter x12 -> x0, waiting for transfers between devices: 425 us -> none  [the longest x1 110 us: per_device(): lax.psum_scatter(summed[5], 'dp', scatter_dimension=0, tiled=True)]
    pallas_call x0 -> x2, Pallas kernels: none -> 370 us  [the longest x1 195 us: backward(): pl.pallas_call(functools.partial(bwd_kernel, cfg), name='backward_reduce'...]
    all_gather x12 -> x0, waiting for transfers between devices: 285 us -> none  [the longest x4 81.3 us: full_rows(): return lax.all_gather(piece, 'mp', axis=1, tiled=True)]
    dot_general x36 -> x0, matrix products: 166 us -> none  [the longest x2 20 us: per_device(): jnp.einsum('bsd,df->bsf', grad_branch, w_down, preferred_element_type=jnp...]
    psum x3 -> x0, blocking collectives: 84.4 us -> none  [the longest x1 39.7 us: per_device(): lax.psum(jnp.sum(keep_local).astype(jnp.float32), ('dp', 'mp'))]
    unnamed x2 -> x0, blocking collectives: 67.9 us -> none
    convert_element_type x11 -> x2, other arithmetic: 48.5 us -> 4.65 us  [the longest x1 3.25 us: per_device(): grad_in.astype(F32)]
    reduce_sum x12 -> x1, other arithmetic: 19.3 us -> 0.01 us  [per_device(): total = jnp.sum(stats, axis=0)]
  transfers between devices with their start and end apart: 24 -> 0, of which waited for: 19 -> 0; matrix products, arithmetic and copies ran while one was open for 20% -> 0% of each run, Pallas kernels for 0% -> 0%
where the time goes in v1:
time: 391 us
  Pallas kernels  370 us (95%)
  local copies, waits for them, and re-layouts  11.5 us (3%)
  other arithmetic  5.37 us (1%)
    pallas_call x1, Pallas kernels, backward(): pl.pallas_call(functools.partial(bwd_kernel, cfg), name='backward_reduce'...  195 us
    pallas_call x1, Pallas kernels, forward(): pl.pallas_call(functools.partial(fwd_kernel, cfg), name='gather_forward',...  175 us

profile of v1, /device:TPU:0, one launch (start us, length us, event | category | flops | bytes accessed | tf_op | source)
XLA Modules:
  0.0 390.6 jit_solution(221981476821159657)
XLA Ops:
  0.6 0.7 tile.4
  1.3 0.1 broadcast_in_dim_tile.6
  1.4 0.7 tile.5
  2.0 0.1 broadcast_in_dim_tile.7
  2.1 1.4 fusion
  4.2 0.1 pad.2.clone
  4.3 0.7 maximum_maximum_fusion.small
  5.0 0.6 broadcast_in_dim.22.krow
  5.6 1.1 broadcast_in_dim.23.kcol
  6.7 1.6 copy.25
  8.3 175.0 %gather_forward.1 = (bf16[24,2,4,2,2,64,256]{6,5,4,3,2,1,0:T(8,128)(2,1)}, bf16[2,512,640]{2,1,0:T(8,128)(2,1)}, bf16[6,2,2,320,256]{4,3,2,1,0:T(8,128)(2,1)}, f...) custom-call(bf16[4,160,1024]{2,1,0:T(8,128)(2,1)} %xin.1, ...), custom_call_target="tpu_custom_call" | custom-call | tf_op jit(solution)/shard_map/gather_forward/pallas_call | solution.py:415
  183.2 194.9 %backward_reduce.1 = (bf16[4,160,1024]{2,1,0:T(8,128)(2,1)}, bf16[4,160,1024]{2,1,0:T(8,128)(2,1)}, f32[24,64,256]{2,1,0:T(8,128)}, f32[4,8,1024]{2,1,0:T(8,128)}) custom-call(bf16[24,2,4,2,2,64,256]{6,5,4,3,2,1,0:T(8,128)(2,1)} %get-tuple-element.29.wg, bf16[2,512,640]{2,1,0:T(8,128)(2,1)} %get-tuple-element.30.at_i, ...), custom_call_target="tpu_custom_call" | custom-call | tf_op jit(solution)/shard_map/backward_reduce/pallas_call | solution.py:871
  378.1 0.0 copy-start
  378.2 3.2 convert_element_type.19
  381.4 0.0 copy-done
  381.4 0.1 slice_bitcast_fusion
  381.5 0.0 copy-start.2
  381.5 0.8 copy.28
  382.4 0.8 copy.29
  383.2 0.0 copy-start.1
  383.2 0.0 copy-done.2
  383.2 0.5 slice.32
  383.7 1.2 slice.25
  386.3 0.8 copy.26
  387.1 0.7 copy.27
  387.8 0.1 constant_dynamic-slice_fusion
  387.8 0.5 slice_bitcast_fusion.3
  388.4 0.0 copy-done.1
  388.4 1.1 copy.31
  (5 shorter events, 0.1 us)
Async XLA Ops:
  378.1 3.3 copy-start
  381.5 1.7 copy-start.2
  383.2 5.2 %copy-start.1 = (bf16[4,160,1024]{2,1,0:T(8,128)(2,1)S(1)}, bf16[4,160,1024]{2,1,0:T(8,128)(2,1)}, u32[]{:S(2)}) copy-start(bf16[4,160,1024]{2,1,0:T(8,128)(2,1)} %get-tuple-element.66) | copy-start | bytes 3932164

commit v2 on v1

--- a/solution.py
+++ b/solution.py
@@ -12,7 +12,9 @@
 EPS = 1e-06
 F32 = jnp.float32
 BF = jnp.bfloat16
-L1, L3, L4, L5 = 2, 1, 1, 1
+PIECES = 5
+T_FIRST = 6
+L1, L3, L4, L5 = 4, 1, 1, 1
 RDY = L3 + L4 + L5
 NT = (((1,), (1,)), ((), ()))
 NN = (((1,), (0,)), ((), ()))
@@ -61,7 +63,7 @@
 
 
 def both_first(k):
-    return (k < 5) | (lax.rem(k, 4) == 1)
+    return (k < PIECES) | ((k >= T_FIRST) & (k < T_FIRST + PIECES))
 
 
 def when(cond, body):
@@ -75,7 +77,7 @@
 def fwd_kernel(cfg, xin, tin, wq, wo, wu, wd, small, krow, kcol, *refs):
     (wg_o, at_o, proj_o, lse_o, o_o, h_o, bnt_o, g_o, gp_o, gy_o, gm_o, gmt_o, out_o, xs_o, ts_o, sm_o, loss_o,
      wg, xs, ts, sm, a, proj, o, lse, h, bn, g, gp, zb, y, tb,
-     local_sem, send_sem, recv_sem, extra_send, extra_recv, out_sem, misc_sem) = refs
+     local_sem, send_sem, recv_sem, extra_send, extra_recv, piece_send, piece_recv, out_sem, misc_sem) = refs
     H, R = cfg["groups"], cfg["rows"]
     NQ, NO, NF = cfg["nq"], cfg["no"], cfg["nf"]
     NCH = NQ + NO + 2 * NF
@@ -144,11 +146,31 @@
         remote(wg.at[k, :, :, :, 1 - c], k, H + 2, place.over_c()).wait_recv()
         keep_chunk(k).start()
 
+    PR = HALF // PIECES
+
+    def piece(i, n, to):
+        src, dst = ((xin, xs), (tin, ts))[i]
+        return pltpu.make_async_remote_copy(
+            src.at[pl.ds(IMG * (1 - x), IMG), pl.ds(PR * n, PR)], dst.at[:, pl.ds(HALF * to + PR * n, PR)],
+            piece_send.at[i, n], piece_recv.at[i, n], device_id=place.over_x(), device_id_type=MESH
+        )
+
+    def piece_at(t):
+        for i, first in ((0, 0), (1, T_FIRST)):
+            n = t - first
+            when((0 <= n < PIECES) if isinstance(n, int) else (n >= 0) & (n < PIECES),
+                 lambda i=i, n=n: piece(i, n, x).start())
+
+    def pieces_in(i):
+        for n in range(PIECES):
+            piece(i, n, 1 - x).wait_recv()
+
     def step(t):
         def inside(k):
             return (0 <= k < NCH) if isinstance(k, int) else (k >= 0) & (k < NCH)
 
         when(inside(t + L1), lambda: s1(t + L1))
+        piece_at(t)
         when(inside(t), lambda: s2(t))
         when(inside(t - L3), lambda: s3(t - L3))
         when(inside(t - L3 - L4), lambda: s4(t - L3 - L4))
@@ -176,14 +198,11 @@
     tl.start()
     sl.start()
     meet(place)
-    xr = extra(xin.at[pl.ds(IMG * (1 - x), IMG)], xs.at[:, mine], 0, place.over_x())
-    tr = extra(tin.at[pl.ds(IMG * (1 - x), IMG)], ts.at[:, mine], 1, place.over_x())
     sl.wait()
     for j in range(1, H):
         extra(sm.at[z, yy, c], sm.at[z, yy, c], 3 + j, place.far(j)).start()
     for k in range(L1):
         s1(k)
-    xr.start()
     for j in range(1, H):
         extra(sm.at[z, yy, c], sm.at[lax.rem(z + H - j, H), yy, c], 3 + j, place.far(j)).wait_recv()
     extra(sm.at[:, yy, c], sm.at[:, yy, c], 2, place.over_y()).start()
@@ -195,7 +214,9 @@
     totals = jnp.sum(sm[...].reshape(H * 4, 8, D), axis=0)
     sm_o[...] = totals
     xl.wait()
-    extra(xin.at[pl.ds(IMG * (1 - x), IMG)], xs.at[:, pl.ds(HALF * (1 - x), HALF)], 0, place.over_x()).wait_recv()
+    for t in range(2, PIECES):
+        step(t)
+    pieces_in(0)
     keep(xs, xs_o)
 
     RB = 32
@@ -221,7 +242,6 @@
             for p in range(2):
                 dst[p, pl.ds(pl.multiple_of(d * 64, 64), 64)] = t[:, p].reshape(64, TOK).astype(BF)
 
-    step(2)
     transposed(a, tb)
     keep(tb, at_o)
 
@@ -256,10 +276,12 @@
         o[group, half, i] = total.astype(BF)
         lse[group, half, i] = logs
 
+    done = PIECES
     for k in range(3):
-        step(k + RDY)
+        while done <= k + RDY:
+            step(done)
+            done += 1
         project(k)
-    done = 3 + RDY
     for group in range(GRP):
         if group:
             for k in range(3 * group, 3 * group + 3):
@@ -297,7 +319,6 @@
         at = pl.ds(pl.multiple_of(r * RB, RB), RB)
         bn[at] = norm_to(h[at], sm_o[1:2])
 
-    tr.start()
     first_up = NQ + NO
 
     def gelu(k, half):
@@ -337,7 +358,7 @@
             y[...] += dot(g[k, half], chunk(first_down + k, half), NT)
 
     tl.wait()
-    extra(tin.at[pl.ds(IMG * (1 - x), IMG)], ts.at[:, pl.ds(HALF * (1 - x), HALF)], 1, place.over_x()).wait_recv()
+    pieces_in(1)
     keep(ts, ts_o)
     loss_o[...] = jnp.zeros_like(loss_o)
     factor = 2.0 * cfg["tokens"] / sm_o[2:3]
@@ -370,8 +391,9 @@
     for n, copy in enumerate(kept):
         if n not in (0, 1, 8):
             copy.wait()
-    xr.wait_send()
-    tr.wait_send()
+    for i in range(2):
+        for n in range(PIECES):
+            piece(i, n, x).wait_send()
     for j in range(1, H):
         extra(sm.at[z, yy, c], sm.at[z, yy, c], 3 + j, place.far(j)).wait_send()
     extra(sm.at[:, yy, c], sm.at[:, yy, c], 2, place.over_y()).wait_send()
@@ -427,7 +449,8 @@
             pltpu.VMEM(lhs, BF),
             pltpu.SemaphoreType.DMA((NCH,)), pltpu.SemaphoreType.DMA((NCH, H + 3)),
             pltpu.SemaphoreType.DMA((NCH, H + 3)), pltpu.SemaphoreType.DMA((H + 4,)),
-            pltpu.SemaphoreType.DMA((H + 4,)), pltpu.SemaphoreType.DMA((NCH,)), pltpu.SemaphoreType.DMA((32,)),
+            pltpu.SemaphoreType.DMA((H + 4,)), pltpu.SemaphoreType.DMA((2, PIECES)),
+            pltpu.SemaphoreType.DMA((2, PIECES)), pltpu.SemaphoreType.DMA((NCH,)), pltpu.SemaphoreType.DMA((32,)),
         ],
         compiler_params=pltpu.CompilerParams(
             collective_id=0, has_side_effects=True, vmem_limit_bytes=63 * 2**20
@@ -469,14 +492,31 @@
 
 SLOTS = 3
 WSLOTS = 4
-LAGS = (1, 4, 7, 9)
+CALLS = (
+    (0, 0, 0, 0, 0), (0, 0, 0, 0, 0), (0, 0, 0, 0, 0), (1, 0, 0, 0, 0), (0, 0, 0, 0, 0),
+    (1, 0, 0, 0, 0), (0, 0, 0, 0, 0), (1, 0, 0, 0, 0), (0, 1, 0, 0, 0), (1, 0, 0, 0, 0),
+    (0, 1, 0, 0, 0), (1, 0, 0, 0, 0), (0, 0, 0, 0, 0), (1, 0, 0, 0, 0), (0, 1, 0, 0, 0),
+    (1, 0, 0, 0, 0), (0, 0, 0, 0, 0), (1, 0, 0, 0, 0), (0, 0, 2, 0, 0), (1, 1, 1, 0, 0),
+    (1, 0, 0, 0, 0), (0, 0, 0, 0, 0), (0, 0, 0, 0, 0), (1, 1, 0, 1, 0), (0, 0, 0, 0, 0),
+    (1, 0, 0, 1, 0), (0, 0, 0, 0, 0), (1, 1, 1, 1, 0), (1, 0, 0, 0, 0), (0, 1, 0, 0, 0),
+    (0, 0, 0, 0, 0), (1, 1, 0, 0, 0), (1, 0, 0, 1, 0), (0, 1, 1, 0, 0), (0, 1, 0, 0, 0),
+    (0, 0, 0, 0, 0), (0, 0, 0, 0, 0), (1, 0, 0, 0, 0), (0, 1, 0, 0, 0), (1, 0, 3, 1, 0),
+    (0, 1, 3, 0, 0), (0, 1, 0, 1, 0), (0, 1, 1, 1, 0), (0, 0, 0, 0, 0), (0, 0, 1, 1, 0),
+    (0, 1, 0, 0, 0), (1, 0, 0, 1, 0), (1, 0, 1, 0, 0), (1, 1, 0, 1, 0), (0, 1, 1, 1, 0),
+    (0, 0, 1, 1, 0), (0, 1, 1, 1, 0), (0, 1, 0, 2, 0), (0, 0, 0, 0, 0), (0, 1, 1, 1, 0),
+    (0, 0, 0, 0, 0), (1, 0, 0, 1, 0), (1, 0, 1, 0, 0), (1, 1, 1, 0, 0), (0, 1, 0, 1, 0),
+)
+DRAIN = (
+    3, 2, 1, 4, 3, 4, 1, 3, 4, 2, 2, 2, 4, 3, 3, 3, 4,
+)
+OUT_FIRST = 1
 
 
 def bwd_kernel(cfg, wg, at_i, proj_i, lse_i, o_i, h_i, bnt_i, g_i, gp_i, gy_i, gm_i, gmt_i, out_i, xs_i,
                totals, loss_i, krow, *refs):
     (out_o, ig_o, dw_o, stat_o,
      q, snd, rcv, near, farr, dw, wb, gb_buf, gpb, gz, zb, gm, lhs1, lhs2, acc, gh, h, o, go, proj, lse, xb, stat, sbuf,
-     core_send, core_recv, credit, near_send, near_recv, far_send, far_recv, extra_send, extra_recv,
+     core_send, core_recv, credit, near_send, near_recv, far_send, far_recv, extra_send, extra_recv, piece_send, piece_recv,
      wsem, gsem, misc_sem, dw_sem) = refs
     H, R = cfg["groups"], cfg["rows"]
     NQ, NO, NF = cfg["nq"], cfg["no"], cfg["nf"]
@@ -493,8 +533,9 @@
         ff = jnp.where(lax.rem(p, 2) == 0, NQ + NO + NF + p // 2, NQ + NO + p // 2)
         return jnp.where(p < 2 * NF, ff, jnp.where(p < 2 * NF + NO, p - 2 * NF + NQ, p - 2 * NF - NO))
 
-    def relay(k):
-        first = jnp.where(both_first(k), 1, 1 - c)
+    def relay(p):
+        both = (p >= OUT_FIRST) & (p < OUT_FIRST + PIECES)
+        first = jnp.where(both, 1, 1 - c)
         xa = jnp.where(first == 1, 1 - x, x)
         ya = jnp.where(first == 1, yy, 1 - yy)
         return xa, ya, jnp.where(first == 1, x, 1 - x), jnp.where(first == 1, 1 - yy, yy)
@@ -589,20 +630,20 @@
         pl.when(p + SLOTS < NCH)(
             lambda: pl.semaphore_signal(credit, 1, device_id=place.over_c(), device_id_type=MESH)
         )
-        xa, ya, xo, yo = relay(k)
+        xa, ya, xo, yo = relay(p)
         near_copy(q.at[k, 1 - x, :, 1 - yy], k, 0, place.at(z, yo, c, xo)).start()
         near_copy(q.at[k, xo, :, yo], k, 1, place.at(z, yo, c, xo)).start()
 
     def r2(p):
         k = ident(p)
-        xa, ya, xo, yo = relay(k)
+        xa, ya, xo, yo = relay(p)
         near_copy(q.at[k, 1 - x, :, 1 - yy], k, 0, place.at(z, yo, c, xo)).wait_recv()
         added(k, xa, ya, (0,))
         near_copy(q.at[k, xa, :, ya], k, 2, place.at(z, ya, c, xa)).start()
 
     def r3(p):
         k = ident(p)
-        xa, ya, xo, yo = relay(k)
+        xa, ya, xo, yo = relay(p)
         near_copy(q.at[k, xo, :, yo], k, 1, place.at(z, yo, c, xo)).wait_recv()
         near_copy(q.at[k, xa, :, ya], k, 2, place.at(z, ya, c, xa)).wait_recv()
         added(k, x, yy, (1, 2))
@@ -623,14 +664,35 @@
 
     stages = (r1, r2, r3, r4)
 
-    def tick(p, lags=LAGS):
-        for stage, lag in zip(stages, lags):
-            n = p - lag
-            if isinstance(n, int):
-                if 0 <= n < NCH:
-                    stage(jnp.int32(n))
-            else:
-                pl.when((n >= 0) & (n < NCH))(lambda stage=stage, n=n: stage(n))
+    before = [[sum(call[i] for call in CALLS[:n]) for n in range(len(CALLS) + 1)] for i in range(5)]
+    place_no = [0]
+
+    def pick(table, index):
+        value = jnp.int32(table[0])
+        for n in range(1, len(table)):
+            if table[n] != table[n - 1]:
+                value = jnp.where(index >= n, table[n], value)
+        return value
+
+    def serve(numbers, index=None):
+        for i in (3, 2, 1, 0):
+            counts = [CALLS[n][i] for n in numbers]
+            starts = [before[i][n] for n in numbers]
+            if index is None:
+                for n in range(counts[0]):
+                    stages[i](jnp.int32(starts[0] + n))
+            elif max(counts) == 1:
+                pl.when(pick(counts, index) > 0)(lambda i=i, starts=starts: stages[i](pick(starts, index)))
+            elif max(counts) > 1:
+                first = pick(starts, index)
+
+                @pl.loop(first, first + pick(counts, index))
+                def _(n, i=i):
+                    stages[i](n)
+
+    def serve_next():
+        serve([place_no[0]])
+        place_no[0] += 1
 
     gm_l.wait()
     gmt_l.wait()
@@ -643,17 +705,31 @@
         pl.when(n + WSLOTS < NCH)(lambda: wload(n + WSLOTS).start())
 
     GB = 64
+    PR = HALF // PIECES
+    mine = pl.ds(HALF * x, HALF)
+
+    def piece(i, n):
+        return pltpu.make_async_remote_copy(
+            xb.at[:, pl.ds(HALF * (1 - x) + PR * n, PR)],
+            (out_o, ig_o)[i].at[pl.ds(IMG * x, IMG), pl.ds(PR * n, PR)],
+            piece_send.at[i, n], piece_recv.at[i, n], device_id=place.over_x(), device_id_type=MESH
+        )
+
     acc[...] = jnp.zeros_like(acc)
+    out_l.wait()
+    out_c = pltpu.make_async_copy(xb.at[:, mine], out_o.at[pl.ds(IMG * x, IMG)], misc_sem.at[30])
+    out_c.start()
 
     @pl.loop(0, NF)
     def _(j):
         s = lax.rem(j, 2)
+        pl.when(j < PIECES)(lambda: piece(0, j).start())
         gl, gpl = gload(j)
         gl.wait()
         produce(2 * j, lhs1, lambda half: gb_buf[s, half])
+        serve([4 * n for n in range(NF)], j)
         gpl.wait()
         wload(2 * j).wait()
-        tick(2 * j)
 
         @pl.loop(0, 2)
         def _(half):
@@ -671,8 +747,9 @@
             for copy in gload(j + 2):
                 copy.start()
 
+        serve([4 * n + 1 for n in range(NF)], j)
         produce(2 * j + 1, lhs2, lambda half: gz[half])
-        tick(2 * j + 1)
+        serve([4 * n + 2 for n in range(NF)], j)
         wload(2 * j + 1).wait()
 
         @pl.loop(0, 2)
@@ -680,14 +757,9 @@
             acc[...] += dot(gz[half], wchunk(2 * j + 1, half), NT)
 
         wnext(2 * j + 1)
-
-    mine, other = pl.ds(HALF * x, HALF), pl.ds(HALF * (1 - x), HALF)
-    out_l.wait()
-    out_r = extra(xb.at[:, other], out_o.at[pl.ds(IMG * x, IMG)], 0, place.over_x())
-    out_r.start()
-    out_c = pltpu.make_async_copy(xb.at[:, mine], out_o.at[pl.ds(IMG * x, IMG)], misc_sem.at[30])
-    out_c.start()
-
+        serve([4 * n + 3 for n in range(NF)], j)
+
+    place_no[0] = 4 * NF
     RB = 32
 
     def norm_back(values, grad, gain):
@@ -703,18 +775,24 @@
     def fold(v):
         return jnp.sum(v.reshape(RB // 8, 8, D), axis=0)
 
+    base = 2 * NF
     stat[...] = jnp.zeros_like(stat)
     gy_l.wait()
     h_l.wait()
 
-    @pl.loop(0, TOK // RB)
-    def _(r):
-        at = pl.ds(pl.multiple_of(r * RB, RB), RB)
-        back, product = norm_back(h[at], acc[at], totals[1:2])
-        total = gh[at] + back
-        gh[at] = total
-        gm[at] = total.astype(BF)
-        stat[1] += fold(product)
+    for part in range(2):
+        count = TOK // RB // 2
+
+        @pl.loop(part * count, (part + 1) * count)
+        def _(r):
+            at = pl.ds(pl.multiple_of(r * RB, RB), RB)
+            back, product = norm_back(h[at], acc[at], totals[1:2])
+            total = gh[at] + back
+            gh[at] = total
+            gm[at] = total.astype(BF)
+            stat[1] += fold(product)
+
+        serve_next()
 
     def transposed(src, dst):
         @pl.loop(0, D // 128)
@@ -727,10 +805,9 @@
     at_l = load(at_i, lhs2)
     transposed(gm, lhs1)
     o_l.wait()
-    base = 2 * NF
     for k in range(NO):
         produce(jnp.int32(base + k), lhs1, lambda half, k=k: o[k, half].reshape(TOK, CW))
-        tick(base + k)
+        serve_next()
         wload(jnp.int32(base + k)).wait()
 
         @pl.loop(0, 2)
@@ -738,6 +815,7 @@
             go[k, half] = dot(gm[...], wchunk(jnp.int32(base + k), half)).astype(BF).reshape(IMG, SEQ, CW)
 
         wnext(jnp.int32(base + k))
+        serve_next()
     proj_l.wait()
     lse_l.wait()
     lane = lax.broadcasted_iota(jnp.int32, (SEQ, CW), 1) // HDIM
@@ -772,29 +850,26 @@
     acc[...] = jnp.zeros_like(acc)
     at_l.wait()
     out_c.wait()
-    out_r.wait_send()
+    for n in range(PIECES):
+        piece(0, n).wait_send()
     xs_l = load(xs_i, xb)
-    pos = [base + NO - lag for lag in LAGS]
-
-    def advance(n, upto):
-        for i, stage in enumerate(stages):
-            for _ in range(n):
-                if pos[i] < upto:
-                    stage(jnp.int32(pos[i]))
-                    pos[i] += 1
 
     for group in range(GRP):
-        for i in range(1):
-            advance(1, base + NO + 3 * group)
+        numbers = [place_no[0] + u for u in range(2 * IMG)]
+        place_no[0] += 2 * IMG
 
         @pl.loop(0, 2 * IMG)
-        def _(u, group=group):
+        def _(u, numbers=numbers, group=group):
+            serve(numbers, u)
             attend_back(group, u)
+
+        for k in range(3 * group, 3 * group + 3):
+            serve_next()
+            produce(jnp.int32(base + NO + k), lhs2, lambda half, k=k: proj[k, half].reshape(TOK, CW))
 
         for k in range(3 * group, 3 * group + 3):
             p = base + NO + k
-            produce(jnp.int32(p), lhs2, lambda half, k=k: proj[k, half].reshape(TOK, CW))
-            advance(2, p)
+            serve_next()
             wload(jnp.int32(p)).wait()
 
             @pl.loop(0, 2)
@@ -804,19 +879,31 @@
             wnext(jnp.int32(p))
 
     xs_l.wait()
-    advance(2, NCH)
-
-    @pl.loop(0, TOK // RB)
-    def _(r):
-        at = pl.ds(pl.multiple_of(r * RB, RB), RB)
-        per = SEQ // RB
-        img, row = r // per, pl.multiple_of(lax.rem(r, per) * RB, RB)
+    serve_next()
+    per = SEQ // RB
+
+    def finish(img, row):
+        at = pl.ds(pl.multiple_of(img * SEQ + row, RB), RB)
         back, product = norm_back(xb[img, pl.ds(row, RB)].astype(F32), acc[at], totals[0:1])
         xb[img, pl.ds(row, RB)] = (gh[at] + back).astype(BF)
         stat[0] += fold(product)
 
-    ig_r = extra(xb.at[:, other], ig_o.at[pl.ds(IMG * x, IMG)], 1, place.over_x())
-    ig_r.start()
+    @pl.loop(0, PIECES)
+    def _(n):
+        @pl.loop(0, IMG)
+        def _(img):
+            finish(img, pl.multiple_of(HALF * (1 - x) + PR * n, RB))
+
+        piece(1, n).start()
+
+    serve_next()
+
+    @pl.loop(0, PIECES)
+    def _(n):
+        @pl.loop(0, IMG)
+        def _(img):
+            finish(img, pl.multiple_of(HALF * x + PR * n, RB))
+
     ig_c = pltpu.make_async_copy(xb.at[:, mine], ig_o.at[pl.ds(IMG * x, IMG)], misc_sem.at[31])
     ig_c.start()
 
@@ -824,25 +911,36 @@
     small = jnp.where(row == 0, jnp.sum(stat[0], axis=0, keepdims=True),
                       jnp.where(row == 1, jnp.sum(stat[1], axis=0, keepdims=True),
                                 jnp.tile(loss_i[...], (1, D // 128))))
-    for n, partner in enumerate((place.over_c(), place.over_y(), place.over_x())):
-        sbuf[2 * n] = small
-        copy = extra(sbuf.at[2 * n], sbuf.at[2 * n + 1], 2 + n, partner)
-        copy.start()
-        advance(2, NCH)
-        copy.wait()
-        small = small + sbuf[2 * n + 1]
-    stat_o[z] = small
-    for j in range(1, H):
-        extra(stat_o.at[z], stat_o.at[z], 4 + j, place.far(j)).start()
-    while pos[-1] < NCH:
-        advance(1, NCH)
-    for j in range(1, H):
-        copy = extra(stat_o.at[z], stat_o.at[lax.rem(z + H - j, H)], 4 + j, place.far(j))
-        copy.wait()
-
-    out_r.wait_recv()
-    ig_r.wait()
+    steps = (place.over_c(), place.over_y(), place.over_x())
+
+    def small_sum(n):
+        if 1 <= n <= 3:
+            extra(sbuf.at[2 * n - 2], sbuf.at[2 * n - 1], 1 + n, steps[n - 1]).wait()
+        value = small if n == 0 else sbuf[2 * n - 2] + sbuf[2 * n - 1] if n < 4 else None
+        if n < 3:
+            sbuf[2 * n] = value
+            extra(sbuf.at[2 * n], sbuf.at[2 * n + 1], 2 + n, steps[n]).start()
+        elif n == 3:
+            stat_o[z] = value
+            for j in range(1, H):
+                extra(stat_o.at[z], stat_o.at[z], 4 + j, place.far(j)).start()
+        else:
+            for j in range(1, H):
+                extra(stat_o.at[z], stat_o.at[lax.rem(z + H - j, H)], 4 + j, place.far(j)).wait()
+
+    done = [before[i][len(CALLS)] for i in range(5)]
+    for i in DRAIN:
+        if i < 4:
+            stages[i](jnp.int32(done[i]))
+        else:
+            small_sum(done[i])
+        done[i] += 1
+    assert done == [NCH] * 4 + [5] and place_no[0] == len(CALLS)
+
     ig_c.wait()
+    for n in range(PIECES):
+        piece(0, n).wait_recv()
+        piece(1, n).wait()
 
     @pl.loop(NCH - SLOTS, NCH)
     def _(p):
@@ -885,7 +983,7 @@
             vm((TOK, D), F32), vm((TOK, D), F32), vm((TOK, D), F32), vm(o.shape, BF), vm(o.shape, BF),
             vm(proj.shape, BF), vm(lse.shape, F32), vm(xs.shape, BF), vm((2, 8, D), F32), vm((6, 8, D), F32),
             dma((NCH,)), dma((NCH,)), pltpu.SemaphoreType.REGULAR, dma((NCH, 3)), dma((NCH, 3)),
-            dma((NCH, H - 1)), dma((NCH, H - 1)), dma((H + 4,)), dma((H + 4,)),
+            dma((NCH, H - 1)), dma((NCH, H - 1)), dma((H + 4,)), dma((H + 4,)), dma((2, PIECES)), dma((2, PIECES)),
             dma((NCH,)), dma((NF, 2)), dma((32,)), dma((NCH,)),
         ],
         compiler_params=pltpu.CompilerParams(

time: 391 us -> 324 us (0.83)
  Pallas kernels: 370 us -> 303 us
    pallas_call x1, Pallas kernels: 195 us -> 146 us  [backward(): pl.pallas_call(functools.partial(bwd_kernel, cfg), name='backward_reduce'...]
    pallas_call x1, Pallas kernels: 175 us -> 157 us  [forward(): pl.pallas_call(functools.partial(fwd_kernel, cfg), name='gather_forward',...]
where the time goes in v2:
time: 324 us; the launch traced here: 323 us
  Pallas kernels  303 us (94%)
  local copies, waits for them, and re-layouts  11.5 us (4%)
  other arithmetic  5.37 us (2%)
  between operations  3.84 us (1%)
    pallas_call x1, Pallas kernels, forward(): pl.pallas_call(functools.partial(fwd_kernel, cfg), name='gather_forward',...  157 us
    pallas_call x1, Pallas kernels, backward(): pl.pallas_call(functools.partial(bwd_kernel, cfg), name='backward_reduce'...  146 us

profile of v2, /device:TPU:0, one launch (start us, length us, event | category | flops | bytes accessed | tf_op | source)
XLA Modules:
  0.0 323.4 jit_solution(17639748852745872801)
XLA Ops:
  0.6 0.7 tile.4
  1.3 0.1 broadcast_in_dim_tile.6
  1.4 0.7 tile.5
  2.0 0.1 broadcast_in_dim_tile.7
  2.1 1.4 fusion
  4.2 0.1 pad.2.clone
  4.3 0.7 maximum_maximum_fusion.small
  5.0 0.6 broadcast_in_dim.22.krow
  5.6 1.1 broadcast_in_dim.23.kcol
  6.7 1.6 copy.25
  8.3 156.9 %gather_forward.1 = (bf16[24,2,4,2,2,64,256]{6,5,4,3,2,1,0:T(8,128)(2,1)}, bf16[2,512,640]{2,1,0:T(8,128)(2,1)}, bf16[6,2,2,320,256]{4,3,2,1,0:T(8,128)(2,1)}, f...) custom-call(bf16[4,160,1024]{2,1,0:T(8,128)(2,1)} %xin.1, ...), custom_call_target="tpu_custom_call" | custom-call | tf_op jit(solution)/shard_map/gather_forward/pallas_call | solution.py:437
  165.2 145.8 %backward_reduce.1 = (bf16[4,160,1024]{2,1,0:T(8,128)(2,1)}, bf16[4,160,1024]{2,1,0:T(8,128)(2,1)}, f32[24,64,256]{2,1,0:T(8,128)}, f32[4,8,1024]{2,1,0:T(8,128)}) custom-call(bf16[24,2,4,2,2,64,256]{6,5,4,3,2,1,0:T(8,128)(2,1)} %get-tuple-element.29.wg, bf16[2,512,640]{2,1,0:T(8,128)(2,1)} %get-tuple-element.30.at_i, ...), custom_call_target="tpu_custom_call" | custom-call | tf_op jit(solution)/shard_map/backward_reduce/pallas_call | solution.py:969
  311.0 0.0 copy-start
  311.0 3.2 %convert_element_type.19 = f32[4,160,1024]{2,1,0:T(8,128)} convert(bf16[4,160,1024]{2,1,0:T(8,128)(2,1)} %get-tuple-element.47) | non-fusion elementwise | flops 655360 | bytes 3932160 | tf_op jit(solution)/shard_map/convert_element_type | solution.py:1017
  314.3 0.0 copy-done
  314.3 0.1 slice_bitcast_fusion
  314.4 0.0 copy-start.2
  314.4 0.8 copy.28
  315.2 0.8 copy.29
  316.1 0.0 copy-start.1
  316.1 0.0 copy-done.2
  316.1 0.5 slice.32
  316.6 1.2 slice.25
  319.2 0.8 copy.26
  320.0 0.7 copy.27
  320.6 0.1 constant_dynamic-slice_fusion
  320.7 0.5 slice_bitcast_fusion.3
  321.2 0.0 copy-done.1
  321.2 1.1 copy.31
  (5 shorter events, 0.1 us)
Async XLA Ops:
  311.0 3.3 %copy-start = (f32[24,64,256]{2,1,0:T(8,128)S(1)}, f32[24,64,256]{2,1,0:T(8,128)}, u32[]{:S(2)}) copy-start(f32[24,64,256]{2,1,0:T(8,128)} %get-tuple-element.48) | copy-start | bytes 4718596
  314.4 1.7 copy-start.2
  316.1 5.2 %copy-start.1 = (bf16[4,160,1024]{2,1,0:T(8,128)(2,1)S(1)}, bf16[4,160,1024]{2,1,0:T(8,128)(2,1)}, u32[]{:S(2)}) copy-start(bf16[4,160,1024]{2,1,0:T(8,128)(2,1)} %get-tuple-element.66) | copy-start | bytes 3932164
